TPU v7x, 512 devices: a whole 4x8x8 slice. The times are simulated.
512 devices in a mesh: seq: 32 (over y, x), head: 16 (over z, core).
Axes of the slice: x: 4, y: 8, z: 8, core: 2. Of those that a mesh axis runs over, the one named last changes fastest.
Arguments:
- queries: bfloat16 [8192, 8192], P('seq', 'head'), may hold values from -1.796875 to 1.796875
- key_rows: bfloat16 [8192, 8192], P('seq', 'head'), may hold values from -1.796875 to 1.796875
- value_rows: bfloat16 [8192, 8192], P('seq', 'head'), may hold values from -6 to 6
- level_table: float32 [64, 7, 64], P(None, None, 'head'), may hold values from 0.25 to 4
- level_index: int32 [8192, 7], P('seq'), may hold values from 0 to 63
- norm_gain: float32 [8192], replicated, may hold values from 0.5 to 1.5
- cotangent: bfloat16 [8192, 8192], P(('seq', 'head')), may hold values from -6 to 6
Outputs:
- normed: bfloat16 [8192, 8192], P(('seq', 'head'))
- grad_query: bfloat16 [8192, 8192], P('seq', 'head')
- grad_key: bfloat16 [8192, 8192], P('seq', 'head')
- grad_value: bfloat16 [8192, 8192], P('seq', 'head')
- grad_table: float32 [64, 7, 64], P(None, None, 'head')
- grad_gain: float32 [8192], replicated
All inputs are finite; a program needn't handle non-finite values.
Results may differ from a plain program's by a relative error of at most 0.014.
Values may be sent and summed in bfloat16 or wider, within the bound.
A program may use at most 64 MiB of HBM per device.

v0:
```python
import jax
import jax.numpy as jnp
from jax import lax
from jax.sharding import PartitionSpec as P

CH = 128
LEVELS = 7
TABLE = 64


EPSILON = 1e-06
HIGHEST = lax.Precision.HIGHEST


def swapped(value, axis, bit):
    mask = 2**bit
    pairs = [(source, source ^ mask) for source in range(lax.axis_size(axis))]
    return lax.ppermute(value, axis, pairs)


def bit_length_of(values, places):
    result = jnp.zeros_like(values)
    for exponent in range(places):
        result = result + (values >= 1 << exponent).astype(jnp.int32)
    return result


def level_mask(spans):
    row_ids = lax.broadcasted_iota(jnp.int32, (spans, spans), 0)
    col_ids = lax.broadcasted_iota(jnp.int32, (spans, spans), 1)
    lengths = bit_length_of(jnp.bitwise_xor(row_ids, col_ids), 16)
    stacked = [((lengths == 1) & (col_ids < row_ids)).astype(jnp.float32)]
    return jnp.stack(stacked)


def body(queries, key_rows, value_rows, level_table, level_index, norm_gain, cotangent):
    tok_dev = queries.shape[0]
    head_count = level_table.shape[2]
    head_width = queries.shape[1] // head_count
    spans = tok_dev // CH
    local_bits = spans.bit_length() - 1
    seq_bits = lax.axis_size("seq").bit_length() - 1
    cross_count = LEVELS - 1 - local_bits
    shard_id = lax.axis_index("seq")
    query_blocks = queries.reshape(spans, CH, head_count, head_width)
    key_blocks = key_rows.reshape(spans, CH, head_count, head_width)
    value_blocks = value_rows.reshape(spans, CH, head_count, head_width)
    onehot = (level_index[:, :, None] == jnp.arange(TABLE, dtype=jnp.int32)[None, None, :]).astype(
        jnp.float32
    )
    weights = jnp.einsum("tlx,xlh->tlh", onehot, level_table, precision=HIGHEST)
    weights = weights.reshape(spans, CH, LEVELS, head_count)
    span_states = jnp.einsum(
        "icha,ichb->ihab", key_blocks, value_blocks, preferred_element_type=jnp.float32
    )
    masks_local = level_mask(spans)
    intra_states = jnp.einsum("mij,jhab->imhab", masks_local, span_states, precision=HIGHEST)
    shard_total = jnp.sum(span_states, axis=0)
    state_zeros = jnp.zeros((cross_count, head_count, head_width, head_width), jnp.float32)
    shards_in = lax.all_gather(
        shard_total[None].astype(jnp.bfloat16), "seq", axis=0, tiled=True
    ).astype(jnp.float32)
    source = jnp.arange(shards_in.shape[0], dtype=jnp.int32)
    lengths = bit_length_of(jnp.bitwise_xor(source, shard_id), 16)
    slot_of = jnp.minimum(lengths + local_bits, LEVELS - 1) - local_bits - 1
    selector = (slot_of[:, None] == jnp.arange(cross_count, dtype=jnp.int32)[None, :]) & (
        source < shard_id
    )[:, None]
    cross_states = state_zeros + jnp.einsum(
        "sk,shab->khab", selector.astype(jnp.float32), shards_in, precision=HIGHEST
    )
    spread = jnp.broadcast_to(cross_states[None], (spans,) + cross_states.shape)
    level_states = jnp.concatenate([intra_states, spread], axis=1).astype(jnp.bfloat16)
    far_out = jnp.einsum(
        "icha,ilhab->iclhb", query_blocks, level_states, preferred_element_type=jnp.float32
    )
    row_ids = lax.broadcasted_iota(jnp.int32, (CH, CH), 0)
    col_ids = lax.broadcasted_iota(jnp.int32, (CH, CH), 1)
    causal = col_ids <= row_ids
    scores = jnp.einsum(
        "icha,inha->ihcn", query_blocks, key_blocks, preferred_element_type=jnp.float32
    )
    scores = jnp.where(causal, scores, 0.0)
    near_out = jnp.einsum(
        "ihcn,inhb->ichb",
        scores.astype(jnp.bfloat16),
        value_blocks,
        preferred_element_type=jnp.float32,
    )
    level_out = jnp.concatenate([near_out[:, :, None], far_out], axis=2)
    attn = jnp.sum(weights[..., None] * level_out, axis=2).astype(jnp.bfloat16)
    attn_rows = attn.reshape(tok_dev, head_count * head_width)
    token_attn = lax.all_to_all(attn_rows, "head", split_axis=0, concat_axis=1, tiled=True)
    attn_f = token_attn.astype(jnp.float32)
    inv_rms = lax.rsqrt(jnp.mean(attn_f * attn_f, axis=1, keepdims=True) + EPSILON)
    unit_rows = attn_f * inv_rms
    normed = (unit_rows * norm_gain).astype(jnp.bfloat16)
    grad_out = cotangent.astype(jnp.float32)
    scaled = grad_out * norm_gain
    grad_gain = lax.psum(jnp.sum(grad_out * unit_rows, axis=0), ("seq", "head"))
    grad_attn = (
        (scaled - unit_rows * jnp.mean(scaled * unit_rows, axis=1, keepdims=True)) * inv_rms
    ).astype(jnp.bfloat16)
    head_grad = lax.all_to_all(grad_attn, "head", split_axis=1, concat_axis=0, tiled=True)
    grad_blocks = head_grad.reshape(spans, CH, head_count, head_width)
    grad_f = grad_blocks.astype(jnp.float32)
    grad_weight = jnp.sum(level_out * grad_f[:, :, None], axis=4)
    along_values = jnp.einsum(
        "ichb,inhb->ihcn", grad_blocks, value_blocks, preferred_element_type=jnp.float32
    )
    first_weight = jnp.transpose(weights[:, :, 0, :], (0, 2, 1))[..., None]
    grad_scores = jnp.where(causal, along_values * first_weight, 0.0).astype(jnp.bfloat16)
    weighted_scores = jnp.where(causal, scores * first_weight, 0.0).astype(jnp.bfloat16)
    near_dq = jnp.einsum(
        "ihcn,inha->icha", grad_scores, key_blocks, preferred_element_type=jnp.float32
    )
    near_dk = jnp.einsum(
        "ihcn,icha->inha", grad_scores, query_blocks, preferred_element_type=jnp.float32
    )
    near_dv = jnp.einsum(
        "ihcn,ichb->inhb", weighted_scores, grad_blocks, preferred_element_type=jnp.float32
    )
    far_dq = jnp.einsum(
        "ichb,ilhab->iclha", grad_blocks, level_states, preferred_element_type=jnp.float32
    )
    grad_query = near_dq + jnp.sum(weights[:, :, 1:, :, None] * far_dq, axis=2)
    scaled_grad = (weights[:, :, 1:, :, None] * grad_f[:, :, None]).astype(jnp.bfloat16)
    query_grads = jnp.einsum(
        "icha,iclhb->ilhab", query_blocks, scaled_grad, preferred_element_type=jnp.float32
    )
    inner_grad = jnp.einsum(
        "mij,imhab->jhab", masks_local, query_grads[:, :local_bits], precision=HIGHEST
    )
    shard_grads = jnp.sum(query_grads[:, local_bits:], axis=0)
    cross_grad = jnp.zeros((head_count, head_width, head_width), jnp.float32)
    group_grads = shard_grads
    for bit_pos in range(seq_bits):
        partner = swapped(group_grads.astype(jnp.bfloat16), "seq", bit_pos).astype(
            group_grads.dtype
        )
        lower_half = 1.0 - jnp.bitwise_and(jnp.right_shift(shard_id, bit_pos), 1).astype(
            jnp.float32
        )
        level_slot = min(bit_pos, cross_count - 1)
        cross_grad = cross_grad + lower_half * partner[level_slot]
        group_grads = group_grads + partner
    key_state = (inner_grad + cross_grad[None]).astype(jnp.bfloat16)
    grad_key = near_dk + jnp.einsum(
        "jhab,jnhb->jnha", key_state, value_blocks, preferred_element_type=jnp.float32
    )
    grad_value = near_dv + jnp.einsum(
        "jhab,jnha->jnhb", key_state, key_blocks, preferred_element_type=jnp.float32
    )
    table_part = jnp.einsum(
        "tlx,tlh->xlh", onehot, grad_weight.reshape(tok_dev, LEVELS, head_count), precision=HIGHEST
    )
    grad_table = lax.psum(table_part, "seq")
    row_shape = (tok_dev, head_count * head_width)
    return (
        normed,
        grad_query.astype(jnp.bfloat16).reshape(row_shape),
        grad_key.astype(jnp.bfloat16).reshape(row_shape),
        grad_value.astype(jnp.bfloat16).reshape(row_shape),
        grad_table,
        grad_gain,
    )


def solution(mesh):
    placed = (
        P("seq", "head"),
        P("seq", "head"),
        P("seq", "head"),
        P(None, None, "head"),
        P("seq", None),
        P(),
        P(("seq", "head"), None),
    )
    return jax.shard_map(
        body,
        mesh=mesh,
        in_specs=placed,
        out_specs=(
            P(("seq", "head"), None),
            P("seq", "head"),
            P("seq", "head"),
            P("seq", "head"),
            P(None, None, "head"),
            P(),
        ),
        check_vma=False,
    )
```

profile of v0, /device:TPU:32, one launch (start us, length us, event | category | flops | bytes accessed | tf_op | source)
XLA Modules:
  0.0 519.8 jit_solution(9532326248119924726)
XLA Ops:
  7.2 1.1 reshape.150
  10.7 1.3 fusion.16
  13.8 86.5 %all-gather.3.cloned.1.call-done = bf16[128,128,128]{2,1,0:T(8,128)(2,1)} async-done(((bf16[4,128,128]{2,1,0:T(8,128)(2,1)}), bf16[128,128,128]{2,1,0:T(8,128)(2,1)}) %all-gather.3.cloned.1.call-update) | async-done | bytes 4194320 | tf_op jit(solution)/shard_map/all_gather | solution.py:60
  100.3 4.5 fusion.5
  107.4 1.7 copy-done.1
  110.0 18.5 %all_to_all.26 = bf16[16,16,512]{2,1,0:T(8,128)(2,1)S(1)} all-to-all(bf16[16,16,512]{2,1,0:T(8,128)(2,1)S(1)} %convert_element_type.402), channel_id=1, replica_groups=mesh['seq'=32,'head'=16] {'head'}, dimensions={0} | all-to-all | bytes 524288 | tf_op jit(solution)/shard_map/all_to_all | solution.py:93
  130.7 3.5 all-to-all-start.1
  134.3 11.3 %all-to-all-done.1 = bf16[16,16,512]{2,0,1:T(8,128)(2,1)S(1)} async-done(((bf16[16,16,512]{2,0,1:T(8,128)(2,1)}), bf16[16,16,512]{2,0,1:T(8,128)(2,1)S(1)}, u32[]{:S(2)}, u32[]{:S(2)}) %all-to-all-start.1) | async-done | bytes 262176 | tf_op jit(solution)/shard_map/all_to_all | solution.py:104
  147.7 1.4 copy-done.3
  149.2 2.8 collective-permute-start
  152.0 16.3 %collective-permute-done = bf16[5,4,128,128]{2,3,0,1:T(8,128)(2,1)S(1)} collective-permute-done((bf16[5,4,128,128]{2,3,0,1:T(8,128)(2,1)S(1)}, bf16[5,4,128,128]{2,3,0,1:T(8,128)(2,1)S(1)}, u32[]{:S(2)}, u32[]{:S(2)}) %collective-permute-start) | collective-permute-done | bytes 655392 | tf_op jit(solution)/shard_map/ppermute | solution.py:18
  169.4 4.0 collective-permute-start.1
  173.4 16.0 %collective-permute-done.1 = bf16[5,4,128,128]{2,3,0,1:T(8,128)(2,1)S(1)} collective-permute-done((bf16[5,4,128,128]{2,3,0,1:T(8,128)(2,1)}, bf16[5,4,128,128]{2,3,0,1:T(8,128)(2,1)S(1)}, u32[]{:S(2)}, u32[]{:S(2)}) %collective-permute-start.1) | collective-permute-done | bytes 655392 | tf_op jit(solution)/shard_map/ppermute | solution.py:18
  189.4 1.1 fusion.27
  190.5 4.0 collective-permute-start.2
  194.5 100.7 %psum.15 = f32[8192]{0:T(1024)} all-reduce(f32[8192]{0:T(1024)S(1)} %get-tuple-element.6), channel_id=1, replica_groups=mesh['seq'=32,'head'=16] {'seq','head'}, use_global_device_ids=true, to_apply=%region_9.10 | all-reduce | flops 8192 | bytes 65536 | tf_op jit(solution)/shard_map/psum | solution.py:100
  295.2 3.0 fusion.2
  298.2 2.0 copy.219
  300.3 1.3 fusion.11
  301.6 2.5 fusion.26
  304.0 2.5 collective-permute-start.3
  308.4 1.9 slice_bitcast_fusion
  310.3 2.0 copy.226
  312.3 25.5 %collective-permute-done.3 = bf16[5,4,128,128]{2,3,0,1:T(8,128)(2,1)} collective-permute-done((bf16[5,4,128,128]{2,3,0,1:T(8,128)(2,1)}, bf16[5,4,128,128]{2,3,0,1:T(8,128)(2,1)}, u32[]{:S(2)}, u32[]{:S(2)}) %collective-permute-start.3) | collective-permute-done | bytes 655392 | tf_op jit(solution)/shard_map/ppermute | solution.py:18
  337.8 2.6 add_convert_fusion
  340.4 4.2 collective-permute-start.4
  344.9 157.1 %psum.14 = f32[64,7,4]{0,2,1:T(4,128)} all-reduce(f32[64,7,4]{0,2,1:T(4,128)S(1)} %convolution_bitcast_fusion.7), channel_id=1, replica_groups=mesh['seq'=32,'head'=16] {'seq'}, use_global_device_ids=true, to_apply=%region_7.8 | all-reduce | flops 1792 | bytes 14336 | tf_op jit(solution)/shard_map/psum | solution.py:157
  502.0 2.1 fusion.61
  504.1 2.4 fusion.28
  506.8 1.2 convert_element_type.422
  508.0 1.2 convert_element_type.425
  509.2 1.1 fusion.31
  (95 shorter events, 17.8 us)
Async XLA Ops:
  7.2 3.1 copy-start
  7.2 3.1 copy-start.19
  7.2 3.4 copy-start.17
  7.2 93.1 %all-gather.3.cloned.1.call-start = ((), (), s32[]{:S(2)}) async-start(), calls=%async_computation.2 | async-start | bytes 4325376 | tf_op jit(solution)/shard_map/all_gather | solution.py:60
  12.2 93.5 %copy-start.15 = (bf16[2,1,4,128,128]{3,4,1,2,0:T(8,128)(2,1)}, bf16[2,1,4,128,128]{3,4,1,2,0:T(8,128)(2,1)S(1)}, u32[]{:S(2)}) copy-start(bf16[2,1,4,128,128]{3,4,1,2,0:T(8,128)(2,1)S(1)} %copy.206) | copy-start | bytes 786436
  12.6 0.8 copy-start.5
  13.8 93.6 %copy-start.6 = (f32[2,128,1,4,128]{1,4,2,3,0:T(8,128)}, f32[2,128,1,4,128]{1,4,2,3,0:T(8,128)S(1)}, u32[]{:S(2)}) copy-start(f32[2,128,1,4,128]{1,4,2,3,0:T(8,128)S(1)} %convolution_bitcast_fusion.5) | copy-start | bytes 1572868
  105.8 1.0 copy-start.4
  107.4 1.7 copy-start.1
  109.8 18.9 %copy-start.16 = (bf16[16,8192]{1,0:T(8,128)(2,1)S(1)}, bf16[16,8192]{1,0:T(8,128)(2,1)}, u32[]{:S(2)}) copy-start(bf16[16,8192]{1,0:T(8,128)(2,1)} %param.13) | copy-start | bytes 786436
  109.9 18.9 %copy-start.18 = (f32[8192]{0:T(1024)S(1)}, f32[8192]{0:T(1024)}, u32[]{:S(2)}) copy-start(f32[8192]{0:T(1024)} %param.12) | copy-start | bytes 98308
  130.7 14.9 %all-to-all-start.1 = ((bf16[16,16,512]{2,0,1:T(8,128)(2,1)}), bf16[16,16,512]{2,0,1:T(8,128)(2,1)S(1)}, u32[]{:S(2)}, u32[]{:S(2)}) async-start(bf16[16,16,512]{2,0,1:T(8,128)(2,1)} %bitcast.93), calls=%async_computation.1 | async-start | bytes 524288 | tf_op jit(solution)/shard_map/all_to_all | solution.py:104
  145.7 0.7 copy-start.10
  146.6 0.8 copy-start.8
  147.5 1.6 copy-start.3
  149.2 19.2 %collective-permute-start = (bf16[5,4,128,128]{2,3,0,1:T(8,128)(2,1)S(1)}, bf16[5,4,128,128]{2,3,0,1:T(8,128)(2,1)S(1)}, u32[]{:S(2)}, u32[]{:S(2)}) collective-permute-start(bf16[5,4,128,128]{2,3,0,1:T(8,128)(2,1)S(1)} %convert_element_type.415), channel_id=1, source_target_pairs={{0,16},{16,0},{32,48},{48,32},{64,80},{80,64},{96,112},{112,96},{1... | collective-permute-start | bytes 1966088 | tf_op jit(solution)/shard_map/ppermute | solution.py:18
  169.4 20.0 %collective-permute-start.1 = (bf16[5,4,128,128]{2,3,0,1:T(8,128)(2,1)}, bf16[5,4,128,128]{2,3,0,1:T(8,128)(2,1)S(1)}, u32[]{:S(2)}, u32[]{:S(2)}) collective-permute-start(bf16[5,4,128,128]{2,3,0,1:T(8,128)(2,1)} %fusion.56), channel_id=1, source_target_pairs={{0,32},{16,48},{32,0},{48,16},{64,96},{80,112},{96,64},{112,80},{1... | collective-permute-start | bytes 1966088 | tf_op jit(solution)/shard_map/ppermute | solution.py:18
  190.5 111.1 %collective-permute-start.2 = (bf16[5,4,128,128]{2,3,0,1:T(8,128)(2,1)}, bf16[5,4,128,128]{2,3,0,1:T(8,128)(2,1)}, u32[]{:S(2)}, u32[]{:S(2)}) collective-permute-start(bf16[5,4,128,128]{2,3,0,1:T(8,128)(2,1)} %fusion.27), channel_id=1, source_target_pairs={{0,64},{16,80},{32,96},{48,112},{64,0},{80,16},{96,32},{112,48},{1... | collective-permute-start | bytes 1966088 | tf_op jit(solution)/shard_map/ppermute | solution.py:18
  301.5 5.0 copy-start.13
  301.6 5.0 copy-start.12
  301.6 6.1 %copy-start.2 = (f32[2,128,6,4,128]{1,4,2,3,0:T(8,128)S(1)}, f32[2,128,6,4,128]{1,4,2,3,0:T(8,128)}, u32[]{:S(2)}) copy-start(f32[2,128,6,4,128]{1,4,2,3,0:T(8,128)} %copy-done.1) | copy-start | bytes 9437188
  304.0 3.7 copy-start.7
  304.0 3.7 copy-start.9
  304.0 33.8 %collective-permute-start.3 = (bf16[5,4,128,128]{2,3,0,1:T(8,128)(2,1)}, bf16[5,4,128,128]{2,3,0,1:T(8,128)(2,1)}, u32[]{:S(2)}, u32[]{:S(2)}) collective-permute-start(bf16[5,4,128,128]{2,3,0,1:T(8,128)(2,1)} %fusion.26), channel_id=1, source_target_pairs={{0,128},{16,144},{32,160},{48,176},{64,192},{80,208},{96,224},{112... | collective-permute-start | bytes 1966088 | tf_op jit(solution)/shard_map/ppermute | solution.py:18
  340.4 168.8 %collective-permute-start.4 = (bf16[5,4,128,128]{2,3,0,1:T(8,128)(2,1)}, bf16[5,4,128,128]{2,3,0,1:T(8,128)(2,1)}, u32[]{:S(2)}, u32[]{:S(2)}) collective-permute-start(bf16[5,4,128,128]{2,3,0,1:T(8,128)(2,1)} %add_convert_fusion), channel_id=1, source_target_pairs={{0,256},{16,272},{32,288},{48,304},{64,320},{80,336},{96,352},{112... | collective-permute-start | bytes 1966088 | tf_op jit(solution)/shard_map/ppermute | solution.py:18
  509.2 1.5 copy-start.11
  510.4 1.0 copy-start.14
Sparse Core Ops, SparseCore 0:
  11.8 88.4 all-gather.2
where the time goes:
time: 521 us; the launch traced here: 520 us
  blocking collectives  276 us (53%)
  waiting for transfers between devices  156 us (30%)
  starting transfers between devices  21.1 us (4%)
  local copies, waits for them, and re-layouts  19.3 us (4%)
  matrix products  19 us (4%)
  between operations  14.6 us (3%)
  other arithmetic  13.9 us (3%)
    psum x1, blocking collectives, body(): grad_table = lax.psum(table_part, 'seq')  157 us
    psum x1, blocking collectives, body(): grad_gain = lax.psum(jnp.sum(grad_out * unit_rows, axis=0), ('seq', 'head'))  101 us
    all_gather x1, waiting for transfers between devices, body(): lax.all_gather(shard_total[None].astype(jnp.bfloat16), 'seq', axis=0, til...  86.5 us
    ppermute x5, waiting for transfers between devices, swapped(): return lax.ppermute(value, axis, pairs)  57.8 us
    all_to_all x1, blocking collectives, body(): lax.all_to_all(attn_rows, 'head', split_axis=0, concat_axis=1, tiled=True)  18.5 us
    ppermute x5, starting transfers between devices, swapped(): return lax.ppermute(value, axis, pairs)  17.5 us
    all_to_all x1, waiting for transfers between devices, body(): lax.all_to_all(grad_attn, 'head', split_axis=1, concat_axis=0, tiled=True)  11.3 us
  transfers between devices with their start and end apart: 7, of which 5 were waited for; matrix products, arithmetic and copies ran while one was open for 4% of the time, Pallas kernels for 0%

commit v1 on v0

v1 whole, which is shorter than its diff:
```python
import functools

import jax
import jax.numpy as jnp
from jax import lax
from jax.experimental import pallas as pl
from jax.experimental.pallas import tpu as pltpu
from jax.sharding import PartitionSpec as P

CH = 128
DH = 128
EPSILON = 1e-06
MESH = pl.DeviceIdType.MESH
F32 = jnp.float32
BF16 = jnp.bfloat16

NN = (((1,), (0,)), ((), ()))
NT = (((1,), (1,)), ((), ()))
TN = (((0,), (0,)), ((), ()))


def mm(a, b, dims):
    return lax.dot_general(a, b, dims, preferred_element_type=F32)


def split_two(value):
    high = value.astype(BF16)
    low = (value - high.astype(F32)).astype(BF16)
    return high, low


def bit_of(index, place):
    return lax.rem(lax.div(index, jnp.int32(2**place)), jnp.int32(2))


def send(src, dst, send_sem, recv_sem, axis, target):
    pltpu.make_async_remote_copy(
        src_ref=src,
        dst_ref=dst,
        send_sem=send_sem,
        recv_sem=recv_sem,
        device_id={axis: target},
        device_id_type=MESH,
    ).start()


def drain(view, sem):
    pltpu.make_async_copy(view, view, sem).wait()


def kernel(
    shards,
    members,
    q_in,
    k_in,
    v_in,
    tab_in,
    idx_in,
    gain_in,
    cot_in,
    normed_out,
    dq_out,
    dk_out,
    dv_out,
    gtab_out,
    ggain_out,
    q,
    k,
    v,
    tab,
    idx,
    gain,
    cot,
    total,
    total_in,
    level,
    level_in,
    state,
    intra,
    weight,
    out,
    scores,
    attn,
    stat,
    stat_in,
    normed,
    gpart,
    gpart_in,
    gsum,
    gall,
    grad,
    qg,
    qg_in,
    inner,
    ks,
    ks_in,
    dq,
    dk,
    dv,
    dk_bf,
    dv_bf,
    tpart,
    tpart_in,
    tsum,
    load_sem,
    store_sem,
    send_sem,
    recv_sem,
    tab_sem,
):
    me = lax.axis_index("seq")
    mine = lax.axis_index("head")
    bits = shards.bit_length() - 1
    toks, width = q.shape
    heads = width // DH
    levels = bits + 2
    rows = heads * DH // shards
    group = shards // heads
    piece = toks // members
    table = tab.shape[2]
    features = members * width

    def head_cols(h):
        return slice(h * DH, (h + 1) * DH)

    def span_rows(i):
        return slice(i * CH, (i + 1) * CH)

    def seq_peers(step):
        def one(offset, carry):
            step(lax.rem(me + offset, jnp.int32(shards)))
            return carry

        lax.fori_loop(1, shards, one, 0)

    def head_peers(step):
        def one(offset, carry):
            step(lax.rem(mine + offset, jnp.int32(members)))
            return carry

        lax.fori_loop(1, members, one, 0)

    def ones_in(index):
        count = bit_of(index, 0)
        for place in range(1, bits):
            count = count + bit_of(index, place)
        return count

    my_count = ones_in(me)
    my_cols = pl.ds(pl.multiple_of(mine * width, width), width)

    loads = [
        pltpu.make_async_copy(k_in, k, load_sem.at[0]),
        pltpu.make_async_copy(v_in, v, load_sem.at[1]),
        pltpu.make_async_copy(q_in, q, load_sem.at[2]),
        pltpu.make_async_copy(tab_in, tab, load_sem.at[3]),
        pltpu.make_async_copy(idx_in, idx, load_sem.at[4]),
        pltpu.make_async_copy(gain_in.at[:, my_cols], gain, load_sem.at[5]),
        pltpu.make_async_copy(
            cot_in.at[:, my_cols],
            cot.at[pl.ds(pl.multiple_of(mine * piece, piece), piece)],
            load_sem.at[6],
        ),
    ]
    for copy in loads:
        copy.start()

    barrier = pltpu.get_barrier_semaphore()

    def greet_seq(peer):
        pl.semaphore_signal(barrier, inc=1, device_id={"seq": peer}, device_id_type=MESH)

    def greet_head(peer):
        pl.semaphore_signal(barrier, inc=1, device_id={"head": peer}, device_id_type=MESH)

    seq_peers(greet_seq)
    head_peers(greet_head)

    loads[0].wait()
    loads[1].wait()
    for h in range(heads):
        first = mm(k[span_rows(0), head_cols(h)], v[span_rows(0), head_cols(h)], TN)
        second = mm(k[span_rows(1), head_cols(h)], v[span_rows(1), head_cols(h)], TN)
        intra[h] = first.astype(BF16)
        total[h * DH : (h + 1) * DH, :] = (first + second).astype(BF16)

    pl.semaphore_wait(barrier, shards + members - 2)

    def send_total(peer):
        send(
            total.at[pl.ds(pl.multiple_of(peer * rows, rows), rows)],
            total_in.at[me],
            send_sem.at[0],
            recv_sem.at[0],
            "seq",
            peer,
        )

    seq_peers(send_total)

    def send_cot(peer):
        send(
            cot_in.at[:, pl.ds(pl.multiple_of(peer * width, width), width)],
            cot.at[pl.ds(pl.multiple_of(mine * piece, piece), piece)],
            send_sem.at[1],
            recv_sem.at[1],
            "head",
            peer,
        )

    head_peers(send_cot)
    total_in[me] = total[pl.ds(pl.multiple_of(me * rows, rows), rows), :]

    for copy in loads[2:6]:
        copy.wait()
    x_ids = lax.broadcasted_iota(jnp.int32, (table, toks), 0)
    stacked = []
    for l in range(levels):
        onehot = (idx[l : l + 1, :] == x_ids).astype(F32).astype(BF16)
        high, low = split_two(tab[l])
        stacked.append(mm(high, onehot, NN))
        stacked.append(mm(low, onehot, NN))
    pad = 128 - 2 * heads * levels
    stacked.append(jnp.zeros((pad, toks), F32))
    columns = jnp.transpose(jnp.concatenate(stacked, axis=0)).astype(BF16)
    row_ids = lax.broadcasted_iota(jnp.int32, (128, width), 0)
    col_head = lax.broadcasted_iota(jnp.int32, (128, width), 1) // DH
    for l in range(levels):
        base = 2 * heads * l
        pick = (row_ids == base + col_head) | (row_ids == base + heads + col_head)
        weight[l] = mm(columns, pick.astype(F32).astype(BF16), NN)

    causal = lax.broadcasted_iota(jnp.int32, (CH, CH), 1) <= lax.broadcasted_iota(
        jnp.int32, (CH, CH), 0
    )
    for h in range(heads):
        for i in range(2):
            at = (span_rows(i), head_cols(h))
            score = jnp.where(causal, mm(q[at], k[at], NT), 0.0)
            scores[2 * h + i] = score
            out[0, at[0], at[1]] = mm(score.astype(BF16), v[at], NN)
        out[1, span_rows(0), head_cols(h)] = jnp.zeros((CH, DH), F32)
        out[1, span_rows(1), head_cols(h)] = mm(
            q[span_rows(1), head_cols(h)], intra[h], NN
        )

    drain(total_in.at[0 : shards - 1], recv_sem.at[0])
    sums = [[total_in[c].astype(F32) for c in range(shards)]]
    for place in range(1, bits):
        below = sums[-1]
        sums.append([below[2 * j] + below[2 * j + 1] for j in range(len(below) // 2)])
    for c in range(shards):
        slot = 0
        for place in range(bits):
            if (c >> place) & 1:
                level[c * bits + slot] = sums[place][(c >> place) ^ 1].astype(BF16)
                slot += 1

    def send_level(peer):
        count = ones_in(peer)
        for n in range(1, bits + 1):

            @pl.when(count == n)
            def _():
                send(
                    level.at[pl.ds(peer * bits, n)],
                    level_in.at[pl.ds(me * bits, n)],
                    send_sem.at[2],
                    recv_sem.at[2],
                    "seq",
                    peer,
                )

    seq_peers(send_level)
    level_in[pl.ds(me * bits, bits)] = level[pl.ds(me * bits, bits)]
    for n in range(1, bits + 1):

        @pl.when(my_count == n)
        def _():
            drain(level_in.at[0 : (shards - 1) * n], recv_sem.at[2])

    slot = jnp.int32(0)
    slots = []
    for place in range(bits):
        mark = bit_of(me, place)
        slots.append(slot)
        for h in range(heads):

            @pl.when(mark == 1)
            def _():
                for g in range(group):
                    state[h, g * rows : (g + 1) * rows, place * DH : (place + 1) * DH] = level_in[
                        (h * group + g) * bits + slot
                    ]

            @pl.when(mark == 0)
            def _():
                state[h, :, place * DH : (place + 1) * DH] = jnp.zeros((DH, DH), BF16)

        slot = slot + mark

    loads[6].wait()
    drain(cot.at[0 : toks - piece], recv_sem.at[1])
    squares = jnp.zeros((toks, DH), F32)
    crosses = jnp.zeros((toks, DH), F32)
    for h in range(heads):
        cols = head_cols(h)
        far = mm(q[:, cols], state[h], NN)
        value = weight[0, :, cols] * out[0, :, cols] + weight[1, :, cols] * out[1, :, cols]
        for place in range(bits):
            part = far[:, place * DH : (place + 1) * DH]
            out[place + 2, :, cols] = part
            value = value + weight[place + 2, :, cols] * part
        value = value.astype(BF16)
        attn[:, cols] = value
        value = value.astype(F32)
        squares = squares + value * value
        crosses = crosses + cot[:, cols].astype(F32) * gain[:, cols] * value
    one_row = jnp.ones((8, DH), BF16)
    for row, part in enumerate((squares, crosses)):
        high, low = split_two(part)
        both = mm(one_row, high, NT) + mm(one_row, low, NT)
        stat[row : row + 1, :] = both[0:1, :]

    def send_stat(peer):
        send(stat, stat_in.at[mine], send_sem.at[3], recv_sem.at[3], "head", peer)

    head_peers(send_stat)
    stat_in[mine] = stat[...]
    drain(stat_in.at[0 : members - 1], recv_sem.at[3])
    both = stat_in[0]
    for m in range(1, members):
        both = both + stat_in[m]
    inv_row = lax.rsqrt(both[0:1, :] * (1.0 / features) + EPSILON)
    mean_row = both[1:2, :] * inv_row * (1.0 / features)
    inv = jnp.transpose(jnp.broadcast_to(inv_row, (DH, toks)))
    mean = jnp.transpose(jnp.broadcast_to(mean_row, (DH, toks)))

    for h in range(heads):
        cols = head_cols(h)
        unit = attn[:, cols].astype(F32) * inv
        cot_f = cot[:, cols].astype(F32)
        normed[:, cols] = (unit * gain[:, cols]).astype(BF16)
        grad[:, cols] = ((cot_f * gain[:, cols] - unit * mean) * inv).astype(BF16)
        gpart[:, cols] = jnp.sum(cot_f * unit, axis=0, keepdims=True)

    for h in range(heads):
        cols = head_cols(h)
        grad_f = grad[:, cols].astype(F32)
        scaled = [
            (weight[place + 2, :, cols] * grad_f).astype(BF16) for place in range(bits)
        ]
        products = mm(q[:, cols], jnp.concatenate(scaled, axis=1), TN)
        for place in range(bits):

            @pl.when(bit_of(me, place) == 1)
            def _():
                for g in range(group):
                    qg[(h * group + g) * bits + slots[place]] = products[
                        g * rows : (g + 1) * rows, place * DH : (place + 1) * DH
                    ].astype(BF16)

    for n in range(1, bits + 1):

        @pl.when(my_count == n)
        def _():
            def send_qg(peer):
                send(
                    qg.at[pl.ds(peer * bits, n)],
                    qg_in.at[pl.ds(me * bits, n)],
                    send_sem.at[4],
                    recv_sem.at[4],
                    "seq",
                    peer,
                )

            seq_peers(send_qg)

    qg_in[pl.ds(me * bits, bits)] = qg[pl.ds(me * bits, bits)]

    own_rows = pl.ds(pl.multiple_of(mine * piece, piece), piece)

    def send_normed(peer):
        send(
            normed.at[pl.ds(pl.multiple_of(peer * piece, piece), piece)],
            normed_out.at[:, my_cols],
            send_sem.at[5],
            recv_sem.at[5],
            "head",
            peer,
        )

    head_peers(send_normed)
    keep_normed = pltpu.make_async_copy(
        normed.at[own_rows], normed_out.at[:, my_cols], store_sem.at[0]
    )
    keep_normed.start()

    def send_gain(peer):
        send(gpart, gpart_in.at[me], send_sem.at[6], recv_sem.at[6], "seq", peer)

    seq_peers(send_gain)
    gpart_in[me] = gpart[...]

    lane_ids = lax.broadcasted_iota(jnp.int32, (8, width), 1) // DH
    head_rows = (
        (lax.broadcasted_iota(jnp.int32, (8, width), 0) == lane_ids).astype(F32).astype(BF16)
    )
    grad_all = grad[...].astype(F32)
    for l in range(levels):
        onehot = (idx[l : l + 1, :] == x_ids).astype(F32).astype(BF16)
        high, low = split_two(out[l] * grad_all)
        by_row = mm(onehot, high, NN) + mm(onehot, low, NN)
        high, low = split_two(by_row)
        result = mm(head_rows, high, NT) + mm(head_rows, low, NT)
        tpart[l] = result[0:heads, :]
    for l in range(levels):

        @pl.when(me != l)
        def _():
            send(tpart.at[l], tpart_in.at[me], send_sem.at[7], recv_sem.at[7], "seq", l)

        @pl.when(me == l)
        def _():
            tpart_in[me] = tpart[l]

    drain(gpart_in.at[0 : shards - 1], recv_sem.at[6])
    both = gpart_in[0]
    for c in range(1, shards):
        both = both + gpart_in[c]
    gsum[...] = both

    def send_gsum(peer):
        send(gsum, gall.at[:, my_cols], send_sem.at[8], recv_sem.at[8], "head", peer)

    head_peers(send_gsum)
    gall[:, my_cols] = both

    for h in range(heads):
        cols = head_cols(h)
        grad_h = grad[:, cols]
        grad_f = grad_h.astype(F32)
        scaled = [
            (weight[place + 2, :, cols] * grad_f).astype(BF16) for place in range(bits)
        ]
        far = mm(jnp.concatenate(scaled, axis=1), state[h], NT)
        near = (weight[1, span_rows(1), cols] * grad_f[CH:]).astype(BF16)
        inner[h] = mm(q[span_rows(1), cols], near, TN)
        for i in range(2):
            at = (span_rows(i), cols)
            along = mm(grad_h[span_rows(i)], v[at], NT)
            first = weight[0, span_rows(i), cols]
            grad_scores = jnp.where(causal, along * first, 0.0).astype(BF16)
            weighted = (scores[2 * h + i] * first).astype(BF16)
            value = far[span_rows(i)] + mm(grad_scores, k[at], NN)
            if i == 1:
                value = value + mm(near, intra[h], NT)
            dq[at] = value.astype(BF16)
            dk[at] = mm(grad_scores, q[at], TN)
            dv[at] = mm(weighted, grad_h[span_rows(i)], TN)
    for n in range(0, bits + 1):

        @pl.when(my_count == n)
        def _():
            drain(qg_in.at[0 : bits * shards // 2 - n], recv_sem.at[4])

    def slot_of(c, place):
        return bin(c & ((1 << place) - 1)).count("1")

    reach = [None]
    for place in range(bits - 1, -1, -1):
        reach_next = []
        for block, above in enumerate(reach):
            upper = range((2 * block + 1) << place, (2 * block + 2) << place)
            part = functools.reduce(
                lambda a, b: a + b, [qg_in[c * bits + slot_of(c, place)].astype(F32) for c in upper]
            )
            reach_next.append(part if above is None else above + part)
            reach_next.append(above)
        reach = reach_next
    for c in range(shards):
        ks[c] = jnp.zeros((rows, DH), BF16) if reach[c] is None else reach[c].astype(BF16)

    def send_ks(peer):
        send(ks.at[peer], ks_in.at[me], send_sem.at[9], recv_sem.at[9], "seq", peer)

    seq_peers(send_ks)
    ks_in[me] = ks[me]

    for l in range(levels):

        @pl.when(me == l)
        def _():
            drain(tpart_in.at[0 : shards - 1], recv_sem.at[7])
            both = tpart_in[0]
            for c in range(1, shards):
                both = both + tpart_in[c]
            tsum[l] = both

            def send_tsum(peer):
                send(tsum.at[l], tsum.at[l], send_sem.at[10], tab_sem.at[l], "seq", peer)

            seq_peers(send_tsum)

    keep_dq = pltpu.make_async_copy(dq, dq_out, store_sem.at[1])
    keep_dq.start()

    drain(ks_in.at[0 : shards - 1], recv_sem.at[9])
    for h in range(heads):
        cols = head_cols(h)
        cross = ks_in[h * group : (h + 1) * group].reshape(DH, DH)
        for i in range(2):
            at = (span_rows(i), cols)
            key_state = cross
            if i == 0:
                key_state = (cross.astype(F32) + inner[h]).astype(BF16)
            dk_bf[at] = (dk[at] + mm(v[at], key_state, NT)).astype(BF16)
            dv_bf[at] = (dv[at] + mm(k[at], key_state, NN)).astype(BF16)

    stores = [
        pltpu.make_async_copy(dk_bf, dk_out, store_sem.at[2]),
        pltpu.make_async_copy(dv_bf, dv_out, store_sem.at[3]),
    ]
    for copy in stores:
        copy.start()

    drain(gall.at[:, 0 : features - width], recv_sem.at[8])
    for l in range(levels):

        @pl.when(me != l)
        def _():
            drain(tsum.at[l], tab_sem.at[l])

    stores += [
        keep_normed,
        keep_dq,
        pltpu.make_async_copy(gall, ggain_out, store_sem.at[4]),
        pltpu.make_async_copy(tsum, gtab_out, store_sem.at[5]),
    ]
    stores[-2].start()
    stores[-1].start()
    drain(normed_out.at[:, 0 : features - width], recv_sem.at[5])
    drain(total.at[0 : (shards - 1) * rows], send_sem.at[0])
    drain(cot.at[0 : toks - piece], send_sem.at[1])
    drain(stat_in.at[0 : members - 1], send_sem.at[3])
    for n in range(0, bits + 1):

        @pl.when(my_count == n)
        def _():
            drain(level.at[0 : bits * shards // 2 - n], send_sem.at[2])
            if n:
                drain(qg.at[0 : (shards - 1) * n], send_sem.at[4])

    drain(normed.at[0 : toks - piece], send_sem.at[5])
    drain(gpart_in.at[0 : shards - 1], send_sem.at[6])
    drain(gall.at[:, 0 : features - width], send_sem.at[8])
    drain(ks_in.at[0 : shards - 1], send_sem.at[9])

    @pl.when(me < levels)
    def _():
        drain(tpart.at[0 : levels - 1], send_sem.at[7])
        drain(tpart_in.at[0 : shards - 1], send_sem.at[10])

    @pl.when(me >= levels)
    def _():
        drain(tpart, send_sem.at[7])

    for copy in stores:
        copy.wait()


def body(shards, members, queries, key_rows, value_rows, level_table, level_index, norm_gain, cotangent):
    toks, width = queries.shape
    table, levels, heads = level_table.shape
    features = norm_gain.shape[0]
    bits = shards.bit_length() - 1
    rows = heads * DH // shards
    any_space = pl.BlockSpec(memory_space=pl.ANY)
    vmem = pltpu.VMEM
    outs = pl.pallas_call(
        functools.partial(kernel, shards, members),
        out_shape=(
            jax.ShapeDtypeStruct(cotangent.shape, BF16),
            jax.ShapeDtypeStruct((toks, width), BF16),
            jax.ShapeDtypeStruct((toks, width), BF16),
            jax.ShapeDtypeStruct((toks, width), BF16),
            jax.ShapeDtypeStruct((levels, heads, table), F32),
            jax.ShapeDtypeStruct((1, features), F32),
        ),
        in_specs=[any_space] * 7,
        out_specs=[any_space] * 6,
        scratch_shapes=[
            vmem((toks, width), BF16),
            vmem((toks, width), BF16),
            vmem((toks, width), BF16),
            vmem((levels, heads, table), F32),
            vmem((levels, toks), jnp.int32),
            vmem((1, width), F32),
            vmem((toks, width), BF16),
            vmem((heads * DH, DH), BF16),
            vmem((shards, rows, DH), BF16),
            vmem((shards * bits, rows, DH), BF16),
            vmem((shards * bits, rows, DH), BF16),
            vmem((heads, DH, bits * DH), BF16),
            vmem((heads, DH, DH), BF16),
            vmem((levels, toks, width), F32),
            vmem((levels, toks, width), F32),
            vmem((2 * heads, CH, CH), F32),
            vmem((toks, width), BF16),
            vmem((2, toks), F32),
            vmem((members, 2, toks), F32),
            vmem((toks, width), BF16),
            vmem((1, width), F32),
            vmem((shards, 1, width), F32),
            vmem((1, width), F32),
            vmem((1, features), F32),
            vmem((toks, width), BF16),
            vmem((shards * bits, rows, DH), BF16),
            vmem((shards * bits, rows, DH), BF16),
            vmem((heads, DH, DH), F32),
            vmem((shards, rows, DH), BF16),
            vmem((shards, rows, DH), BF16),
            vmem((toks, width), BF16),
            vmem((toks, width), F32),
            vmem((toks, width), F32),
            vmem((toks, width), BF16),
            vmem((toks, width), BF16),
            vmem((levels, heads, table), F32),
            vmem((shards, heads, table), F32),
            vmem((levels, heads, table), F32),
            pltpu.SemaphoreType.DMA((7,)),
            pltpu.SemaphoreType.DMA((6,)),
            pltpu.SemaphoreType.DMA((11,)),
            pltpu.SemaphoreType.DMA((10,)),
            pltpu.SemaphoreType.DMA((levels,)),
        ],
        compiler_params=pltpu.CompilerParams(
            collective_id=0, has_side_effects=True, vmem_limit_bytes=48 * 2**20
        ),
    )(
        queries,
        key_rows,
        value_rows,
        jnp.transpose(level_table, (1, 2, 0)),
        jnp.transpose(level_index),
        norm_gain.reshape(1, features),
        cotangent,
    )
    normed, dq, dk, dv, gtab, ggain = outs
    return normed, dq, dk, dv, jnp.transpose(gtab, (2, 0, 1)), ggain.reshape(features)


def solution(mesh):
    wide = P("seq", "head")
    rows = P(("seq", "head"), None)
    table = P(None, None, "head")
    return jax.shard_map(
        functools.partial(body, mesh.shape["seq"], mesh.shape["head"]),
        mesh=mesh,
        in_specs=(wide, wide, wide, table, P("seq", None), P(), rows),
        out_specs=(rows, wide, wide, wide, table, P()),
        check_vma=False,
    )
```

time: 521 us -> 80.5 us (0.15)
  the two profiles are of different devices: /device:TPU:32 before, /device:TPU:48 now
where the time goes in v1:
time: 80.5 us; the launch traced here: 80.1 us
  Pallas kernels  69.4 us (86%)
  local copies, waits for them, and re-layouts  9.98 us (12%)
    pallas_call x1, Pallas kernels, body(): pl.pallas_call(functools.partial(kernel, shards, members), out_shape=(jax...  69.4 us
    unnamed x20, local copies, waits for them, and re-layouts  9.98 us

profile of v1, /device:TPU:48, one launch (start us, length us, event | category | flops | bytes accessed | tf_op | source)
XLA Modules:
  0.0 80.1 jit_solution(16173449286724440865)
XLA Ops:
  0.6 0.0 copy-start
  0.6 0.9 %copy-done = bf16[256,512]{1,0:T(8,128)(2,1)S(1)} copy-done((bf16[256,512]{1,0:T(8,128)(2,1)S(1)}, bf16[256,512]{1,0:T(8,128)(2,1)}, u32[]{:S(2)}) %copy-start) | copy-done | bytes 262168
  1.6 0.0 copy-start.1
  1.6 0.9 %copy-done.1 = bf16[256,512]{1,0:T(8,128)(2,1)S(1)} copy-done((bf16[256,512]{1,0:T(8,128)(2,1)S(1)}, bf16[256,512]{1,0:T(8,128)(2,1)}, u32[]{:S(2)}) %copy-start.1) | copy-done | bytes 262168
  2.5 0.0 copy-start.2
  2.5 0.9 %copy-done.2 = bf16[256,512]{1,0:T(8,128)(2,1)S(1)} copy-done((bf16[256,512]{1,0:T(8,128)(2,1)S(1)}, bf16[256,512]{1,0:T(8,128)(2,1)}, u32[]{:S(2)}) %copy-start.2) | copy-done | bytes 262168
  3.5 0.0 copy-start.3
  3.5 0.9 %copy-done.3 = bf16[16,8192]{1,0:T(8,128)(2,1)S(1)} copy-done((bf16[16,8192]{1,0:T(8,128)(2,1)S(1)}, bf16[16,8192]{1,0:T(8,128)(2,1)}, u32[]{:S(2)}) %copy-start.3) | copy-done | bytes 262168
  4.4 0.0 copy-start.4
  4.4 0.8 copy-done.4
  5.2 0.0 copy-start.5
  5.2 0.7 copy-done.5
  5.9 0.0 copy-start.6
  5.9 0.7 copy-done.6
  6.6 69.4 %shard_map.118 = (bf16[16,8192]{1,0:T(8,128)(2,1)S(1)}, bf16[256,512]{1,0:T(8,128)(2,1)S(1)}, bf16[256,512]{1,0:T(8,128)(2,1)S(1)}, bf16[256,512]{1,0:T(8,128)(2...) custom-call(bf16[256,512]{1,0:T(8,128)(2,1)S(1)} %copy-done, bf16[256,512]{1,0:T(8,128)(2,1)S(1)} %copy-done.1, ...), custom_call_target="tpu_custom_call" | custom-call | tf_op jit(solution)/shard_map/pallas_call | solution.py:580
  76.0 0.7 copy.19
  76.7 0.7 copy.20
  77.4 0.7 copy.21
  78.2 0.7 copy.22
  78.9 0.6 copy.23
  79.5 0.6 copy.24
Async XLA Ops:
  0.6 1.0 %copy-start = (bf16[256,512]{1,0:T(8,128)(2,1)S(1)}, bf16[256,512]{1,0:T(8,128)(2,1)}, u32[]{:S(2)}) copy-start(bf16[256,512]{1,0:T(8,128)(2,1)} %q_in.1) | copy-start | bytes 786436
  1.6 0.9 %copy-start.1 = (bf16[256,512]{1,0:T(8,128)(2,1)S(1)}, bf16[256,512]{1,0:T(8,128)(2,1)}, u32[]{:S(2)}) copy-start(bf16[256,512]{1,0:T(8,128)(2,1)} %k_in.1) | copy-start | bytes 786436
  2.5 0.9 %copy-start.2 = (bf16[256,512]{1,0:T(8,128)(2,1)S(1)}, bf16[256,512]{1,0:T(8,128)(2,1)}, u32[]{:S(2)}) copy-start(bf16[256,512]{1,0:T(8,128)(2,1)} %v_in.1) | copy-start | bytes 786436
  3.5 0.9 %copy-start.3 = (bf16[16,8192]{1,0:T(8,128)(2,1)S(1)}, bf16[16,8192]{1,0:T(8,128)(2,1)}, u32[]{:S(2)}) copy-start(bf16[16,8192]{1,0:T(8,128)(2,1)} %cot_in.1) | copy-start | bytes 786436
  4.4 0.8 copy-start.4
  5.2 0.7 copy-start.5
  5.9 0.7 copy-start.6

commit v2 on v1

--- a/solution.py
+++ b/solution.py
@@ -10,6 +10,8 @@
 CH = 128
 DH = 128
 EPSILON = 1e-06
+NX = 4
+VMEM_BYTES = 48 * 2**20
 MESH = pl.DeviceIdType.MESH
 F32 = jnp.float32
 BF16 = jnp.bfloat16
@@ -59,11 +61,11 @@
     gain_in,
     cot_in,
     normed_out,
-    dq_out,
-    dk_out,
-    dv_out,
-    gtab_out,
-    ggain_out,
+    dq,
+    dk_bf,
+    dv_bf,
+    tsum,
+    gall,
     q,
     k,
     v,
@@ -87,23 +89,21 @@
     gpart,
     gpart_in,
     gsum,
-    gall,
     grad,
     qg,
     qg_in,
     inner,
     ks,
     ks_in,
-    dq,
     dk,
     dv,
-    dk_bf,
-    dv_bf,
     tpart,
     tpart_in,
-    tsum,
+    near,
+    goal,
+    weighted,
+    scaled,
     load_sem,
-    store_sem,
     send_sem,
     recv_sem,
     tab_sem,
@@ -126,19 +126,27 @@
     def span_rows(i):
         return slice(i * CH, (i + 1) * CH)
 
+    def from_far(index, count):
+        step = lax.rem(index, jnp.int32(2))
+        return count // 2 + (1 - 2 * step) * lax.div(index + 1, jnp.int32(2))
+
     def seq_peers(step):
-        def one(offset, carry):
-            step(lax.rem(me + offset, jnp.int32(shards)))
+        def one(index, carry):
+            down = lax.div(me, jnp.int32(NX)) + from_far(lax.div(index, jnp.int32(NX)), shards // NX)
+            across = lax.rem(me, jnp.int32(NX)) + from_far(lax.rem(index, jnp.int32(NX)), NX)
+            step(lax.rem(down, jnp.int32(shards // NX)) * NX + lax.rem(across, jnp.int32(NX)))
             return carry
 
-        lax.fori_loop(1, shards, one, 0)
+        lax.fori_loop(0, shards - 1, one, 0)
 
     def head_peers(step):
-        def one(offset, carry):
-            step(lax.rem(mine + offset, jnp.int32(members)))
+        def one(index, carry):
+            along = lax.div(mine, jnp.int32(2)) + from_far(lax.div(index, jnp.int32(2)), members // 2)
+            core = lax.rem(mine, jnp.int32(2)) + from_far(lax.rem(index, jnp.int32(2)), 2)
+            step(lax.rem(along, jnp.int32(members // 2)) * 2 + lax.rem(core, jnp.int32(2)))
             return carry
 
-        lax.fori_loop(1, members, one, 0)
+        lax.fori_loop(0, members - 1, one, 0)
 
     def ones_in(index):
         count = bit_of(index, 0)
@@ -273,6 +281,18 @@
 
     seq_peers(send_level)
     level_in[pl.ds(me * bits, bits)] = level[pl.ds(me * bits, bits)]
+
+    loads[6].wait()
+    drain(cot.at[0 : toks - piece], recv_sem.at[1])
+    for h in range(heads):
+        cols = head_cols(h)
+        near[:, cols] = weight[0, :, cols] * out[0, :, cols] + weight[1, :, cols] * out[1, :, cols]
+        goal[:, cols] = cot[:, cols].astype(F32) * gain[:, cols]
+        for i in range(2):
+            weighted[2 * h + i] = (
+                scores[2 * h + i] * weight[0, span_rows(i), cols]
+            ).astype(BF16)
+
     for n in range(1, bits + 1):
 
         @pl.when(my_count == n)
@@ -299,14 +319,12 @@
 
         slot = slot + mark
 
-    loads[6].wait()
-    drain(cot.at[0 : toks - piece], recv_sem.at[1])
     squares = jnp.zeros((toks, DH), F32)
     crosses = jnp.zeros((toks, DH), F32)
     for h in range(heads):
         cols = head_cols(h)
         far = mm(q[:, cols], state[h], NN)
-        value = weight[0, :, cols] * out[0, :, cols] + weight[1, :, cols] * out[1, :, cols]
+        value = near[:, cols]
         for place in range(bits):
             part = far[:, place * DH : (place + 1) * DH]
             out[place + 2, :, cols] = part
@@ -315,7 +333,7 @@
         attn[:, cols] = value
         value = value.astype(F32)
         squares = squares + value * value
-        crosses = crosses + cot[:, cols].astype(F32) * gain[:, cols] * value
+        crosses = crosses + goal[:, cols] * value
     one_row = jnp.ones((8, DH), BF16)
     for row, part in enumerate((squares, crosses)):
         high, low = split_two(part)
@@ -339,18 +357,14 @@
     for h in range(heads):
         cols = head_cols(h)
         unit = attn[:, cols].astype(F32) * inv
-        cot_f = cot[:, cols].astype(F32)
-        normed[:, cols] = (unit * gain[:, cols]).astype(BF16)
-        grad[:, cols] = ((cot_f * gain[:, cols] - unit * mean) * inv).astype(BF16)
-        gpart[:, cols] = jnp.sum(cot_f * unit, axis=0, keepdims=True)
-
-    for h in range(heads):
-        cols = head_cols(h)
-        grad_f = grad[:, cols].astype(F32)
-        scaled = [
-            (weight[place + 2, :, cols] * grad_f).astype(BF16) for place in range(bits)
-        ]
-        products = mm(q[:, cols], jnp.concatenate(scaled, axis=1), TN)
+        grad_h = ((goal[:, cols] - unit * mean) * inv).astype(BF16)
+        grad[:, cols] = grad_h
+        grad_f = grad_h.astype(F32)
+        for place in range(bits):
+            scaled[h, :, place * DH : (place + 1) * DH] = (
+                weight[place + 2, :, cols] * grad_f
+            ).astype(BF16)
+        products = mm(q[:, cols], scaled[h], TN)
         for place in range(bits):
 
             @pl.when(bit_of(me, place) == 1)
@@ -377,30 +391,6 @@
             seq_peers(send_qg)
 
     qg_in[pl.ds(me * bits, bits)] = qg[pl.ds(me * bits, bits)]
-
-    own_rows = pl.ds(pl.multiple_of(mine * piece, piece), piece)
-
-    def send_normed(peer):
-        send(
-            normed.at[pl.ds(pl.multiple_of(peer * piece, piece), piece)],
-            normed_out.at[:, my_cols],
-            send_sem.at[5],
-            recv_sem.at[5],
-            "head",
-            peer,
-        )
-
-    head_peers(send_normed)
-    keep_normed = pltpu.make_async_copy(
-        normed.at[own_rows], normed_out.at[:, my_cols], store_sem.at[0]
-    )
-    keep_normed.start()
-
-    def send_gain(peer):
-        send(gpart, gpart_in.at[me], send_sem.at[6], recv_sem.at[6], "seq", peer)
-
-    seq_peers(send_gain)
-    gpart_in[me] = gpart[...]
 
     lane_ids = lax.broadcasted_iota(jnp.int32, (8, width), 1) // DH
     head_rows = (
@@ -424,40 +414,49 @@
         def _():
             tpart_in[me] = tpart[l]
 
-    drain(gpart_in.at[0 : shards - 1], recv_sem.at[6])
-    both = gpart_in[0]
-    for c in range(1, shards):
-        both = both + gpart_in[c]
-    gsum[...] = both
-
-    def send_gsum(peer):
-        send(gsum, gall.at[:, my_cols], send_sem.at[8], recv_sem.at[8], "head", peer)
-
-    head_peers(send_gsum)
-    gall[:, my_cols] = both
+    for h in range(heads):
+        cols = head_cols(h)
+        unit = attn[:, cols].astype(F32) * inv
+        normed[:, cols] = (unit * gain[:, cols]).astype(BF16)
+        gpart[:, cols] = jnp.sum(cot[:, cols].astype(F32) * unit, axis=0, keepdims=True)
+
+    def send_gain(peer):
+        send(gpart, gpart_in.at[me], send_sem.at[6], recv_sem.at[6], "seq", peer)
+
+    seq_peers(send_gain)
+    gpart_in[me] = gpart[...]
+
+    def send_normed(peer):
+        send(
+            normed.at[pl.ds(pl.multiple_of(peer * piece, piece), piece)],
+            normed_out.at[:, my_cols],
+            send_sem.at[5],
+            recv_sem.at[5],
+            "head",
+            peer,
+        )
+
+    head_peers(send_normed)
+    normed_out[:, my_cols] = normed[pl.ds(pl.multiple_of(mine * piece, piece), piece), :]
 
     for h in range(heads):
         cols = head_cols(h)
         grad_h = grad[:, cols]
-        grad_f = grad_h.astype(F32)
-        scaled = [
-            (weight[place + 2, :, cols] * grad_f).astype(BF16) for place in range(bits)
-        ]
-        far = mm(jnp.concatenate(scaled, axis=1), state[h], NT)
-        near = (weight[1, span_rows(1), cols] * grad_f[CH:]).astype(BF16)
-        inner[h] = mm(q[span_rows(1), cols], near, TN)
+        far = mm(scaled[h], state[h], NT)
+        within = (weight[1, span_rows(1), cols] * grad_h[CH:].astype(F32)).astype(BF16)
+        inner[h] = mm(q[span_rows(1), cols], within, TN)
         for i in range(2):
             at = (span_rows(i), cols)
             along = mm(grad_h[span_rows(i)], v[at], NT)
             first = weight[0, span_rows(i), cols]
             grad_scores = jnp.where(causal, along * first, 0.0).astype(BF16)
-            weighted = (scores[2 * h + i] * first).astype(BF16)
             value = far[span_rows(i)] + mm(grad_scores, k[at], NN)
             if i == 1:
-                value = value + mm(near, intra[h], NT)
+                value = value + mm(within, intra[h], NT)
             dq[at] = value.astype(BF16)
             dk[at] = mm(grad_scores, q[at], TN)
-            dv[at] = mm(weighted, grad_h[span_rows(i)], TN)
+            dv[at] = mm(weighted[2 * h + i], grad_h[span_rows(i)], TN)
+
     for n in range(0, bits + 1):
 
         @pl.when(my_count == n)
@@ -473,7 +472,8 @@
         for block, above in enumerate(reach):
             upper = range((2 * block + 1) << place, (2 * block + 2) << place)
             part = functools.reduce(
-                lambda a, b: a + b, [qg_in[c * bits + slot_of(c, place)].astype(F32) for c in upper]
+                lambda a, b: a + b,
+                [qg_in[c * bits + slot_of(c, place)].astype(F32) for c in upper],
             )
             reach_next.append(part if above is None else above + part)
             reach_next.append(above)
@@ -487,6 +487,18 @@
     seq_peers(send_ks)
     ks_in[me] = ks[me]
 
+    drain(gpart_in.at[0 : shards - 1], recv_sem.at[6])
+    both = gpart_in[0]
+    for c in range(1, shards):
+        both = both + gpart_in[c]
+    gsum[...] = both
+
+    def send_gsum(peer):
+        send(gsum, gall.at[:, my_cols], send_sem.at[8], recv_sem.at[8], "head", peer)
+
+    head_peers(send_gsum)
+    gall[:, my_cols] = both
+
     for l in range(levels):
 
         @pl.when(me == l)
@@ -501,9 +513,6 @@
                 send(tsum.at[l], tsum.at[l], send_sem.at[10], tab_sem.at[l], "seq", peer)
 
             seq_peers(send_tsum)
-
-    keep_dq = pltpu.make_async_copy(dq, dq_out, store_sem.at[1])
-    keep_dq.start()
 
     drain(ks_in.at[0 : shards - 1], recv_sem.at[9])
     for h in range(heads):
@@ -517,13 +526,6 @@
             dk_bf[at] = (dk[at] + mm(v[at], key_state, NT)).astype(BF16)
             dv_bf[at] = (dv[at] + mm(k[at], key_state, NN)).astype(BF16)
 
-    stores = [
-        pltpu.make_async_copy(dk_bf, dk_out, store_sem.at[2]),
-        pltpu.make_async_copy(dv_bf, dv_out, store_sem.at[3]),
-    ]
-    for copy in stores:
-        copy.start()
-
     drain(gall.at[:, 0 : features - width], recv_sem.at[8])
     for l in range(levels):
 
@@ -531,14 +533,6 @@
         def _():
             drain(tsum.at[l], tab_sem.at[l])
 
-    stores += [
-        keep_normed,
-        keep_dq,
-        pltpu.make_async_copy(gall, ggain_out, store_sem.at[4]),
-        pltpu.make_async_copy(tsum, gtab_out, store_sem.at[5]),
-    ]
-    stores[-2].start()
-    stores[-1].start()
     drain(normed_out.at[:, 0 : features - width], recv_sem.at[5])
     drain(total.at[0 : (shards - 1) * rows], send_sem.at[0])
     drain(cot.at[0 : toks - piece], send_sem.at[1])
@@ -565,7 +559,16 @@
     def _():
         drain(tpart, send_sem.at[7])
 
-    for copy in stores:
+
+def copy_kernel(*refs):
+    count = len(refs) // 2
+    sems = refs[-1]
+    copies = [
+        pltpu.make_async_copy(refs[i], refs[count + i], sems.at[i]) for i in range(count)
+    ]
+    for copy in copies:
+        copy.start()
+    for copy in copies:
         copy.wait()
 
 
@@ -575,7 +578,7 @@
     features = norm_gain.shape[0]
     bits = shards.bit_length() - 1
     rows = heads * DH // shards
-    any_space = pl.BlockSpec(memory_space=pl.ANY)
+    anywhere = pl.BlockSpec(memory_space=pl.ANY)
     vmem = pltpu.VMEM
     outs = pl.pallas_call(
         functools.partial(kernel, shards, members),
@@ -587,8 +590,8 @@
             jax.ShapeDtypeStruct((levels, heads, table), F32),
             jax.ShapeDtypeStruct((1, features), F32),
         ),
-        in_specs=[any_space] * 7,
-        out_specs=[any_space] * 6,
+        in_specs=[anywhere] * 7,
+        out_specs=[pl.BlockSpec(memory_space=pltpu.VMEM)] * 6,
         scratch_shapes=[
             vmem((toks, width), BF16),
             vmem((toks, width), BF16),
@@ -613,40 +616,50 @@
             vmem((1, width), F32),
             vmem((shards, 1, width), F32),
             vmem((1, width), F32),
-            vmem((1, features), F32),
             vmem((toks, width), BF16),
             vmem((shards * bits, rows, DH), BF16),
             vmem((shards * bits, rows, DH), BF16),
             vmem((heads, DH, DH), F32),
             vmem((shards, rows, DH), BF16),
             vmem((shards, rows, DH), BF16),
-            vmem((toks, width), BF16),
             vmem((toks, width), F32),
             vmem((toks, width), F32),
-            vmem((toks, width), BF16),
-            vmem((toks, width), BF16),
             vmem((levels, heads, table), F32),
             vmem((shards, heads, table), F32),
-            vmem((levels, heads, table), F32),
+            vmem((toks, width), F32),
+            vmem((toks, width), F32),
+            vmem((2 * heads, CH, CH), BF16),
+            vmem((heads, toks, bits * DH), BF16),
             pltpu.SemaphoreType.DMA((7,)),
-            pltpu.SemaphoreType.DMA((6,)),
             pltpu.SemaphoreType.DMA((11,)),
             pltpu.SemaphoreType.DMA((10,)),
             pltpu.SemaphoreType.DMA((levels,)),
         ],
         compiler_params=pltpu.CompilerParams(
-            collective_id=0, has_side_effects=True, vmem_limit_bytes=48 * 2**20
+            collective_id=0, has_side_effects=True, vmem_limit_bytes=VMEM_BYTES
         ),
     )(
-        queries,
-        key_rows,
-        value_rows,
-        jnp.transpose(level_table, (1, 2, 0)),
-        jnp.transpose(level_index),
-        norm_gain.reshape(1, features),
-        cotangent,
+        *(
+            pltpu.with_memory_space_constraint(array, pltpu.HBM)
+            for array in (
+                queries,
+                key_rows,
+                value_rows,
+                jnp.transpose(level_table, (1, 2, 0)),
+                jnp.transpose(level_index),
+                norm_gain.reshape(1, features),
+                cotangent,
+            )
+        )
     )
-    normed, dq, dk, dv, gtab, ggain = outs
+    normed, dq, dk, dv, gtab, ggain = pl.pallas_call(
+        copy_kernel,
+        out_shape=tuple(jax.ShapeDtypeStruct(o.shape, o.dtype) for o in outs),
+        in_specs=[pl.BlockSpec(memory_space=pltpu.VMEM)] * 6,
+        out_specs=[anywhere] * 6,
+        scratch_shapes=[pltpu.SemaphoreType.DMA((6,))],
+        compiler_params=pltpu.CompilerParams(vmem_limit_bytes=4 * 2**20),
+    )(*outs)
     return normed, dq, dk, dv, jnp.transpose(gtab, (2, 0, 1)), ggain.reshape(features)
 
 

time: 80.5 us -> 67.6 us (0.84)
  the two profiles are of different devices: /device:TPU:48 before, /device:TPU:1 now
where the time goes in v2:
time: 67.6 us; the launch traced here: 67.5 us
  Pallas kernels  66.9 us (99%)
    pallas_call x1, Pallas kernels, body(): pl.pallas_call(functools.partial(kernel, shards, members), out_shape=(jax...  65.9 us

profile of v2, /device:TPU:1, one launch (start us, length us, event | category | flops | bytes accessed | tf_op | source)
XLA Modules:
  0.0 67.5 jit_solution(7534654921689927015)
XLA Ops:
  0.6 65.9 %shard_map.118 = (bf16[16,8192]{1,0:T(8,128)(2,1)S(1)}, bf16[256,512]{1,0:T(8,128)(2,1)S(1)}, bf16[256,512]{1,0:T(8,128)(2,1)S(1)}, bf16[256,512]{1,0:T(8,128)(2...) custom-call(bf16[256,512]{1,0:T(8,128)(2,1)} %q_in.1, bf16[256,512]{1,0:T(8,128)(2,1)} %k_in.1, ...), custom_call_target="tpu_custom_call" | custom-call | tf_op jit(solution)/shard_map/pallas_call | solution.py:583
  66.5 1.0 %shard_map.119 = (bf16[16,8192]{1,0:T(8,128)(2,1)}, bf16[256,512]{1,0:T(8,128)(2,1)}, bf16[256,512]{1,0:T(8,128)(2,1)}, bf16[256,512]{1,0:T(8,128)(2,1)}, f32[7,4,64]{2,1,0:T(4,128)}, /*index=5*/f32[1,8192]{1,0:T(1,128)}) custom-call(bf16[16,8192]{1,0:T(8,128)(2,1)S(1)} %get-tuple-element.18.refs_0_, bf16[256,512]{1,0:T(8,128)(2,1)S(1)} %get-tuple-element.19.refs_1_, ...), custom_call_target="tpu_custom_call" | custom-call | tf_op jit(solution)/shard_map/pallas_call | solution.py:655

commit v3 on v2

--- a/solution.py
+++ b/solution.py
@@ -103,6 +103,15 @@
     goal,
     weighted,
     scaled,
+    row_in,
+    row_level,
+    row_level_in,
+    row_qg,
+    row_qg_in,
+    row_ks,
+    row_ks_in,
+    gline,
+    gline_in,
     load_sem,
     send_sem,
     recv_sem,
@@ -111,6 +120,8 @@
     me = lax.axis_index("seq")
     mine = lax.axis_index("head")
     bits = shards.bit_length() - 1
+    far_bits = bits - 2
+    lines = shards // NX
     toks, width = q.shape
     heads = width // DH
     levels = bits + 2
@@ -132,9 +143,9 @@
 
     def seq_peers(step):
         def one(index, carry):
-            down = lax.div(me, jnp.int32(NX)) + from_far(lax.div(index, jnp.int32(NX)), shards // NX)
-            across = lax.rem(me, jnp.int32(NX)) + from_far(lax.rem(index, jnp.int32(NX)), NX)
-            step(lax.rem(down, jnp.int32(shards // NX)) * NX + lax.rem(across, jnp.int32(NX)))
+            line = lax.div(me, jnp.int32(NX)) + from_far(lax.div(index, jnp.int32(NX)), lines)
+            place = lax.rem(me, jnp.int32(NX)) + from_far(lax.rem(index, jnp.int32(NX)), NX)
+            step(lax.rem(line, jnp.int32(lines)) * NX + lax.rem(place, jnp.int32(NX)))
             return carry
 
         lax.fori_loop(0, shards - 1, one, 0)
@@ -149,12 +160,22 @@
         lax.fori_loop(0, members - 1, one, 0)
 
     def ones_in(index):
-        count = bit_of(index, 0)
-        for place in range(1, bits):
+        count = jnp.int32(0)
+        for place in range(2, bits):
             count = count + bit_of(index, place)
         return count
 
     my_count = ones_in(me)
+    across = lax.rem(me, jnp.int32(NX))
+    down = lax.div(me, jnp.int32(NX))
+    row_count = bit_of(me, 0) + bit_of(me, 1)
+    far_slots = far_bits * shards // 2
+
+    def row_peers(step):
+        for offset in range(1, NX):
+            place = lax.rem(across + offset, jnp.int32(NX))
+            step(place, down * NX + place)
+
     my_cols = pl.ds(pl.multiple_of(mine * width, width), width)
 
     loads = [
@@ -175,14 +196,18 @@
 
     barrier = pltpu.get_barrier_semaphore()
 
-    def greet_seq(peer):
+    def greet_seq(offset, carry):
+        peer = lax.rem(me + offset, jnp.int32(shards))
         pl.semaphore_signal(barrier, inc=1, device_id={"seq": peer}, device_id_type=MESH)
-
-    def greet_head(peer):
+        return carry
+
+    def greet_head(offset, carry):
+        peer = lax.rem(mine + offset, jnp.int32(members))
         pl.semaphore_signal(barrier, inc=1, device_id={"head": peer}, device_id_type=MESH)
-
-    seq_peers(greet_seq)
-    head_peers(greet_head)
+        return carry
+
+    lax.fori_loop(1, shards, greet_seq, 0)
+    lax.fori_loop(1, members, greet_head, 0)
 
     loads[0].wait()
     loads[1].wait()
@@ -206,6 +231,18 @@
 
     seq_peers(send_total)
 
+    def send_row(place, peer):
+        send(
+            total.at[pl.ds(pl.multiple_of(place * DH, DH), DH)],
+            row_in.at[across],
+            send_sem.at[11],
+            recv_sem.at[11],
+            "seq",
+            peer,
+        )
+
+    row_peers(send_row)
+
     def send_cot(peer):
         send(
             cot_in.at[:, pl.ds(pl.multiple_of(peer * width, width), width)],
@@ -218,6 +255,7 @@
 
     head_peers(send_cot)
     total_in[me] = total[pl.ds(pl.multiple_of(me * rows, rows), rows), :]
+    row_in[across] = total[pl.ds(pl.multiple_of(across * DH, DH), DH), :]
 
     for copy in loads[2:6]:
         copy.wait()
@@ -253,26 +291,35 @@
         )
 
     drain(total_in.at[0 : shards - 1], recv_sem.at[0])
-    sums = [[total_in[c].astype(F32) for c in range(shards)]]
-    for place in range(1, bits):
+    sums = [
+        functools.reduce(
+            lambda a, b: a + b,
+            [total_in[NX * line + place].astype(F32) for place in range(NX)],
+        )
+        for line in range(lines)
+    ]
+    sums = [sums]
+    for place in range(1, far_bits):
         below = sums[-1]
         sums.append([below[2 * j] + below[2 * j + 1] for j in range(len(below) // 2)])
-    for c in range(shards):
+    for line in range(lines):
         slot = 0
-        for place in range(bits):
-            if (c >> place) & 1:
-                level[c * bits + slot] = sums[place][(c >> place) ^ 1].astype(BF16)
+        for place in range(far_bits):
+            if (line >> place) & 1:
+                block = sums[place][(line >> place) ^ 1].astype(BF16)
+                for c in range(NX * line, NX * line + NX):
+                    level[c * far_bits + slot] = block
                 slot += 1
 
     def send_level(peer):
         count = ones_in(peer)
-        for n in range(1, bits + 1):
+        for n in range(1, far_bits + 1):
 
             @pl.when(count == n)
             def _():
                 send(
-                    level.at[pl.ds(peer * bits, n)],
-                    level_in.at[pl.ds(me * bits, n)],
+                    level.at[pl.ds(peer * far_bits, n)],
+                    level_in.at[pl.ds(me * far_bits, n)],
                     send_sem.at[2],
                     recv_sem.at[2],
                     "seq",
@@ -280,7 +327,31 @@
                 )
 
     seq_peers(send_level)
-    level_in[pl.ds(me * bits, bits)] = level[pl.ds(me * bits, bits)]
+    level_in[pl.ds(me * far_bits, far_bits)] = level[pl.ds(me * far_bits, far_bits)]
+
+    drain(row_in.at[0 : NX - 1], recv_sem.at[11])
+    pair = (row_in[0].astype(F32) + row_in[1].astype(F32)).astype(BF16)
+    row_level[2] = row_in[0]
+    row_level[4] = pair
+    row_level[6] = row_in[2]
+    row_level[7] = pair
+    for place in range(1, NX):
+        n = bin(place).count("1")
+
+        @pl.when(across != place)
+        def _():
+            send(
+                row_level.at[2 * place : 2 * place + n],
+                row_level_in.at[pl.ds(2 * across, n)],
+                send_sem.at[12],
+                recv_sem.at[12],
+                "seq",
+                down * NX + place,
+            )
+
+        @pl.when(across == place)
+        def _():
+            row_level_in[2 * place : 2 * place + n] = row_level[2 * place : 2 * place + n]
 
     loads[6].wait()
     drain(cot.at[0 : toks - piece], recv_sem.at[1])
@@ -293,29 +364,40 @@
                 scores[2 * h + i] * weight[0, span_rows(i), cols]
             ).astype(BF16)
 
-    for n in range(1, bits + 1):
+    for n in range(1, far_bits + 1):
 
         @pl.when(my_count == n)
         def _():
             drain(level_in.at[0 : (shards - 1) * n], recv_sem.at[2])
 
-    slot = jnp.int32(0)
+    for n in (1, 2):
+
+        @pl.when(row_count == n)
+        def _():
+            drain(row_level_in.at[0 : (NX - 1) * n], recv_sem.at[12])
+
     slots = []
     for place in range(bits):
+        if place in (0, 2):
+            slot = jnp.int32(0)
         mark = bit_of(me, place)
         slots.append(slot)
+        lanes = slice(place * DH, (place + 1) * DH)
         for h in range(heads):
 
             @pl.when(mark == 1)
             def _():
-                for g in range(group):
-                    state[h, g * rows : (g + 1) * rows, place * DH : (place + 1) * DH] = level_in[
-                        (h * group + g) * bits + slot
-                    ]
+                if place < 2:
+                    state[h, :, lanes] = row_level_in[2 * h + slot]
+                else:
+                    for g in range(group):
+                        state[h, g * rows : (g + 1) * rows, lanes] = level_in[
+                            (h * group + g) * far_bits + slot
+                        ]
 
             @pl.when(mark == 0)
             def _():
-                state[h, :, place * DH : (place + 1) * DH] = jnp.zeros((DH, DH), BF16)
+                state[h, :, lanes] = jnp.zeros((DH, DH), BF16)
 
         slot = slot + mark
 
@@ -369,19 +451,23 @@
 
             @pl.when(bit_of(me, place) == 1)
             def _():
-                for g in range(group):
-                    qg[(h * group + g) * bits + slots[place]] = products[
-                        g * rows : (g + 1) * rows, place * DH : (place + 1) * DH
-                    ].astype(BF16)
-
-    for n in range(1, bits + 1):
+                part = products[:, place * DH : (place + 1) * DH].astype(BF16)
+                if place < 2:
+                    row_qg[2 * h + slots[place]] = part
+                else:
+                    for g in range(group):
+                        qg[(h * group + g) * far_bits + slots[place]] = part[
+                            g * rows : (g + 1) * rows
+                        ]
+
+    for n in range(1, far_bits + 1):
 
         @pl.when(my_count == n)
         def _():
             def send_qg(peer):
                 send(
-                    qg.at[pl.ds(peer * bits, n)],
-                    qg_in.at[pl.ds(me * bits, n)],
+                    qg.at[pl.ds(peer * far_bits, n)],
+                    qg_in.at[pl.ds(me * far_bits, n)],
                     send_sem.at[4],
                     recv_sem.at[4],
                     "seq",
@@ -390,7 +476,23 @@
 
             seq_peers(send_qg)
 
-    qg_in[pl.ds(me * bits, bits)] = qg[pl.ds(me * bits, bits)]
+    qg_in[pl.ds(me * far_bits, far_bits)] = qg[pl.ds(me * far_bits, far_bits)]
+    for n in (1, 2):
+
+        @pl.when(row_count == n)
+        def _():
+            def send_row_qg(place, peer):
+                send(
+                    row_qg.at[pl.ds(2 * place, n)],
+                    row_qg_in.at[pl.ds(2 * across, n)],
+                    send_sem.at[13],
+                    recv_sem.at[13],
+                    "seq",
+                    peer,
+                )
+
+            row_peers(send_row_qg)
+            row_qg_in[pl.ds(2 * across, n)] = row_qg[pl.ds(2 * across, n)]
 
     lane_ids = lax.broadcasted_iota(jnp.int32, (8, width), 1) // DH
     head_rows = (
@@ -420,11 +522,11 @@
         normed[:, cols] = (unit * gain[:, cols]).astype(BF16)
         gpart[:, cols] = jnp.sum(cot[:, cols].astype(F32) * unit, axis=0, keepdims=True)
 
-    def send_gain(peer):
-        send(gpart, gpart_in.at[me], send_sem.at[6], recv_sem.at[6], "seq", peer)
-
-    seq_peers(send_gain)
-    gpart_in[me] = gpart[...]
+    def send_gain(place, peer):
+        send(gpart, gpart_in.at[across], send_sem.at[6], recv_sem.at[6], "seq", peer)
+
+    row_peers(send_gain)
+    gpart_in[across] = gpart[...]
 
     def send_normed(peer):
         send(
@@ -457,29 +559,52 @@
             dk[at] = mm(grad_scores, q[at], TN)
             dv[at] = mm(weighted[2 * h + i], grad_h[span_rows(i)], TN)
 
-    for n in range(0, bits + 1):
+    drain(gpart_in.at[0 : NX - 1], recv_sem.at[6])
+    both = gpart_in[0]
+    for c in range(1, NX):
+        both = both + gpart_in[c]
+    gline[...] = both
+    gline_in[down] = both
+    for offset in range(1, lines):
+        line = lax.rem(down + offset, jnp.int32(lines))
+        send(
+            gline,
+            gline_in.at[down],
+            send_sem.at[14],
+            recv_sem.at[14],
+            "seq",
+            line * NX + across,
+        )
+
+    for n in range(0, far_bits + 1):
 
         @pl.when(my_count == n)
         def _():
-            drain(qg_in.at[0 : bits * shards // 2 - n], recv_sem.at[4])
-
-    def slot_of(c, place):
-        return bin(c & ((1 << place) - 1)).count("1")
+            drain(qg_in.at[0 : far_slots - n], recv_sem.at[4])
+
+    def slot_of(line, place):
+        return bin(line & ((1 << place) - 1)).count("1")
 
     reach = [None]
-    for place in range(bits - 1, -1, -1):
+    for place in range(far_bits - 1, -1, -1):
         reach_next = []
         for block, above in enumerate(reach):
             upper = range((2 * block + 1) << place, (2 * block + 2) << place)
             part = functools.reduce(
                 lambda a, b: a + b,
-                [qg_in[c * bits + slot_of(c, place)].astype(F32) for c in upper],
+                [
+                    qg_in[c * far_bits + slot_of(line, place)].astype(F32)
+                    for line in upper
+                    for c in range(NX * line, NX * line + NX)
+                ],
             )
             reach_next.append(part if above is None else above + part)
             reach_next.append(above)
         reach = reach_next
-    for c in range(shards):
-        ks[c] = jnp.zeros((rows, DH), BF16) if reach[c] is None else reach[c].astype(BF16)
+    for line in range(lines):
+        block = jnp.zeros((rows, DH), BF16) if reach[line] is None else reach[line].astype(BF16)
+        for c in range(NX * line, NX * line + NX):
+            ks[c] = block
 
     def send_ks(peer):
         send(ks.at[peer], ks_in.at[me], send_sem.at[9], recv_sem.at[9], "seq", peer)
@@ -487,10 +612,41 @@
     seq_peers(send_ks)
     ks_in[me] = ks[me]
 
-    drain(gpart_in.at[0 : shards - 1], recv_sem.at[6])
-    both = gpart_in[0]
-    for c in range(1, shards):
-        both = both + gpart_in[c]
+    for n in (0, 1, 2):
+
+        @pl.when(row_count == n)
+        def _():
+            drain(row_qg_in.at[0 : NX - n], recv_sem.at[13])
+
+    both = row_qg_in[4].astype(F32) + row_qg_in[7].astype(F32)
+    row_ks[0] = (row_qg_in[2].astype(F32) + both).astype(BF16)
+    row_ks[1] = both.astype(BF16)
+    row_ks[2] = row_qg_in[6]
+    row_ks[3] = jnp.zeros((DH, DH), BF16)
+    row_ks_in[across] = row_ks[across]
+    for place in range(NX - 1):
+
+        @pl.when(across != place)
+        def _():
+            send(
+                row_ks.at[place],
+                row_ks_in.at[across],
+                send_sem.at[15],
+                recv_sem.at[15],
+                "seq",
+                down * NX + place,
+            )
+
+    @pl.when(across == NX - 1)
+    def _():
+        for place in range(NX - 1):
+            row_ks_in[place] = jnp.zeros((DH, DH), BF16)
+
+    if lines > 1:
+        drain(gline_in.at[0 : lines - 1], recv_sem.at[14])
+    both = gline_in[0]
+    for c in range(1, lines):
+        both = both + gline_in[c]
     gsum[...] = both
 
     def send_gsum(peer):
@@ -515,14 +671,18 @@
             seq_peers(send_tsum)
 
     drain(ks_in.at[0 : shards - 1], recv_sem.at[9])
+
+    @pl.when(across != NX - 1)
+    def _():
+        drain(row_ks_in.at[0 : NX - 1], recv_sem.at[15])
+
     for h in range(heads):
         cols = head_cols(h)
-        cross = ks_in[h * group : (h + 1) * group].reshape(DH, DH)
+        cross = ks_in[h * group : (h + 1) * group].reshape(DH, DH).astype(F32)
+        cross = cross + row_ks_in[h].astype(F32)
         for i in range(2):
             at = (span_rows(i), cols)
-            key_state = cross
-            if i == 0:
-                key_state = (cross.astype(F32) + inner[h]).astype(BF16)
+            key_state = (cross + inner[h] if i == 0 else cross).astype(BF16)
             dk_bf[at] = (dk[at] + mm(v[at], key_state, NT)).astype(BF16)
             dv_bf[at] = (dv[at] + mm(k[at], key_state, NN)).astype(BF16)
 
@@ -537,16 +697,35 @@
     drain(total.at[0 : (shards - 1) * rows], send_sem.at[0])
     drain(cot.at[0 : toks - piece], send_sem.at[1])
     drain(stat_in.at[0 : members - 1], send_sem.at[3])
-    for n in range(0, bits + 1):
+    for n in range(0, far_bits + 1):
 
         @pl.when(my_count == n)
         def _():
-            drain(level.at[0 : bits * shards // 2 - n], send_sem.at[2])
+            drain(level.at[0 : far_slots - n], send_sem.at[2])
             if n:
                 drain(qg.at[0 : (shards - 1) * n], send_sem.at[4])
 
+    drain(row_in.at[0 : NX - 1], send_sem.at[11])
+    for n in (0, 1, 2):
+
+        @pl.when(row_count == n)
+        def _():
+            drain(row_level.at[0 : NX - n], send_sem.at[12])
+            if n:
+                drain(row_qg.at[0 : (NX - 1) * n], send_sem.at[13])
+
+    @pl.when(across == NX - 1)
+    def _():
+        drain(row_ks.at[0 : NX - 1], send_sem.at[15])
+
+    @pl.when(across != NX - 1)
+    def _():
+        drain(row_ks.at[0 : NX - 2], send_sem.at[15])
+
+    if lines > 1:
+        drain(gline_in.at[0 : lines - 1], send_sem.at[14])
     drain(normed.at[0 : toks - piece], send_sem.at[5])
-    drain(gpart_in.at[0 : shards - 1], send_sem.at[6])
+    drain(gpart_in.at[0 : NX - 1], send_sem.at[6])
     drain(gall.at[:, 0 : features - width], send_sem.at[8])
     drain(ks_in.at[0 : shards - 1], send_sem.at[9])
 
@@ -602,8 +781,8 @@
             vmem((toks, width), BF16),
             vmem((heads * DH, DH), BF16),
             vmem((shards, rows, DH), BF16),
-            vmem((shards * bits, rows, DH), BF16),
-            vmem((shards * bits, rows, DH), BF16),
+            vmem((shards * (bits - 2), rows, DH), BF16),
+            vmem((shards * (bits - 2), rows, DH), BF16),
             vmem((heads, DH, bits * DH), BF16),
             vmem((heads, DH, DH), BF16),
             vmem((levels, toks, width), F32),
@@ -614,11 +793,11 @@
             vmem((members, 2, toks), F32),
             vmem((toks, width), BF16),
             vmem((1, width), F32),
-            vmem((shards, 1, width), F32),
+            vmem((NX, 1, width), F32),
             vmem((1, width), F32),
             vmem((toks, width), BF16),
-            vmem((shards * bits, rows, DH), BF16),
-            vmem((shards * bits, rows, DH), BF16),
+            vmem((shards * (bits - 2), rows, DH), BF16),
+            vmem((shards * (bits - 2), rows, DH), BF16),
             vmem((heads, DH, DH), F32),
             vmem((shards, rows, DH), BF16),
             vmem((shards, rows, DH), BF16),
@@ -630,9 +809,18 @@
             vmem((toks, width), F32),
             vmem((2 * heads, CH, CH), BF16),
             vmem((heads, toks, bits * DH), BF16),
+            vmem((NX, DH, DH), BF16),
+            vmem((2 * NX, DH, DH), BF16),
+            vmem((2 * NX, DH, DH), BF16),
+            vmem((2 * NX, DH, DH), BF16),
+            vmem((2 * NX, DH, DH), BF16),
+            vmem((NX, DH, DH), BF16),
+            vmem((NX, DH, DH), BF16),
+            vmem((1, width), F32),
+            vmem((shards // NX, 1, width), F32),
             pltpu.SemaphoreType.DMA((7,)),
-            pltpu.SemaphoreType.DMA((11,)),
-            pltpu.SemaphoreType.DMA((10,)),
+            pltpu.SemaphoreType.DMA((16,)),
+            pltpu.SemaphoreType.DMA((16,)),
             pltpu.SemaphoreType.DMA((levels,)),
         ],
         compiler_params=pltpu.CompilerParams(

time: 67.6 us -> 57.2 us (0.85)
  Pallas kernels: 66.9 us -> 56.4 us
    pallas_call x1, Pallas kernels: 65.9 us -> 55.4 us  [body(): pl.pallas_call(functools.partial(kernel, shards, members), out_shape=(jax...]
where the time goes in v3:
time: 57.2 us; the launch traced here: 57 us
  Pallas kernels  56.4 us (99%)
  between operations  0.64 us (1%)
    pallas_call x1, Pallas kernels, body(): pl.pallas_call(functools.partial(kernel, shards, members), out_shape=(jax...  55.4 us

profile of v3, /device:TPU:1, one launch (start us, length us, event | category | flops | bytes accessed | tf_op | source)
XLA Modules:
  0.0 57.0 jit_solution(2808394662666940241)
XLA Ops:
  0.6 55.4 %shard_map.118 = (bf16[16,8192]{1,0:T(8,128)(2,1)S(1)}, bf16[256,512]{1,0:T(8,128)(2,1)S(1)}, bf16[256,512]{1,0:T(8,128)(2,1)S(1)}, bf16[256,512]{1,0:T(8,128)(2...) custom-call(bf16[256,512]{1,0:T(8,128)(2,1)} %q_in.1, bf16[256,512]{1,0:T(8,128)(2,1)} %k_in.1, ...), custom_call_target="tpu_custom_call" | custom-call | tf_op jit(solution)/shard_map/pallas_call | solution.py:762
  56.0 1.0 %shard_map.119 = (bf16[16,8192]{1,0:T(8,128)(2,1)}, bf16[256,512]{1,0:T(8,128)(2,1)}, bf16[256,512]{1,0:T(8,128)(2,1)}, bf16[256,512]{1,0:T(8,128)(2,1)}, f32[7,4,64]{2,1,0:T(4,128)}, /*index=5*/f32[1,8192]{1,0:T(1,128)}) custom-call(bf16[16,8192]{1,0:T(8,128)(2,1)S(1)} %get-tuple-element.18.refs_0_, bf16[256,512]{1,0:T(8,128)(2,1)S(1)} %get-tuple-element.19.refs_1_, ...), custom_call_target="tpu_custom_call" | custom-call | tf_op jit(solution)/shard_map/pallas_call | solution.py:843

commit v4 on v3

--- a/solution.py
+++ b/solution.py
@@ -112,6 +112,7 @@
     row_ks_in,
     gline,
     gline_in,
+    q_turned,
     load_sem,
     send_sem,
     recv_sem,
@@ -170,6 +171,7 @@
     down = lax.div(me, jnp.int32(NX))
     row_count = bit_of(me, 0) + bit_of(me, 1)
     far_slots = far_bits * shards // 2
+    owner = [(NX + 1) * l % shards for l in range(levels)]
 
     def row_peers(step):
         for offset in range(1, NX):
@@ -311,22 +313,31 @@
                     level[c * far_bits + slot] = block
                 slot += 1
 
-    def send_level(peer):
-        count = ones_in(peer)
+    def send_line(index, places):
+        line = lax.rem(down + from_far(index, lines), jnp.int32(lines))
+        count = ones_in(line * NX)
         for n in range(1, far_bits + 1):
 
             @pl.when(count == n)
             def _():
-                send(
-                    level.at[pl.ds(peer * far_bits, n)],
-                    level_in.at[pl.ds(me * far_bits, n)],
-                    send_sem.at[2],
-                    recv_sem.at[2],
-                    "seq",
-                    peer,
-                )
-
-    seq_peers(send_level)
+                for i in range(places):
+                    step = 2 - (i + 1) // 2 if i % 2 else 2 + i // 2
+                    peer = line * NX + lax.rem(across + step, jnp.int32(NX))
+                    send(
+                        level.at[pl.ds(peer * far_bits, n)],
+                        level_in.at[pl.ds(me * far_bits, n)],
+                        send_sem.at[2],
+                        recv_sem.at[2],
+                        "seq",
+                        peer,
+                    )
+
+    def whole_line(index, carry):
+        send_line(index, NX)
+        return carry
+
+    lax.fori_loop(0, lines - 1, whole_line, 0)
+    send_line(jnp.int32(lines - 1), NX - 1)
     level_in[pl.ds(me * far_bits, far_bits)] = level[pl.ds(me * far_bits, far_bits)]
 
     drain(row_in.at[0 : NX - 1], recv_sem.at[11])
@@ -359,17 +370,13 @@
         cols = head_cols(h)
         near[:, cols] = weight[0, :, cols] * out[0, :, cols] + weight[1, :, cols] * out[1, :, cols]
         goal[:, cols] = cot[:, cols].astype(F32) * gain[:, cols]
+        q_turned[h] = jnp.transpose(q[:, cols])
         for i in range(2):
             weighted[2 * h + i] = (
                 scores[2 * h + i] * weight[0, span_rows(i), cols]
             ).astype(BF16)
 
-    for n in range(1, far_bits + 1):
-
-        @pl.when(my_count == n)
-        def _():
-            drain(level_in.at[0 : (shards - 1) * n], recv_sem.at[2])
-
+    state[...] = jnp.zeros_like(state)
     for n in (1, 2):
 
         @pl.when(row_count == n)
@@ -380,26 +387,30 @@
     for place in range(bits):
         if place in (0, 2):
             slot = jnp.int32(0)
-        mark = bit_of(me, place)
         slots.append(slot)
-        lanes = slice(place * DH, (place + 1) * DH)
-        for h in range(heads):
-
-            @pl.when(mark == 1)
-            def _():
-                if place < 2:
-                    state[h, :, lanes] = row_level_in[2 * h + slot]
-                else:
-                    for g in range(group):
-                        state[h, g * rows : (g + 1) * rows, lanes] = level_in[
-                            (h * group + g) * far_bits + slot
-                        ]
-
-            @pl.when(mark == 0)
-            def _():
-                state[h, :, lanes] = jnp.zeros((DH, DH), BF16)
-
-        slot = slot + mark
+        slot = slot + bit_of(me, place)
+    for place in (0, 1):
+
+        @pl.when(bit_of(me, place) == 1)
+        def _():
+            for h in range(heads):
+                state[h, :, place * DH : (place + 1) * DH] = row_level_in[2 * h + slots[place]]
+
+    for n in range(1, far_bits + 1):
+
+        @pl.when(my_count == n)
+        def _():
+            drain(level_in.at[0 : (shards - 1) * n], recv_sem.at[2])
+
+    for place in range(2, bits):
+
+        @pl.when(bit_of(me, place) == 1)
+        def _():
+            for h in range(heads):
+                for g in range(group):
+                    state[h, g * rows : (g + 1) * rows, place * DH : (place + 1) * DH] = level_in[
+                        (h * group + g) * far_bits + slots[place]
+                    ]
 
     squares = jnp.zeros((toks, DH), F32)
     crosses = jnp.zeros((toks, DH), F32)
@@ -446,7 +457,7 @@
             scaled[h, :, place * DH : (place + 1) * DH] = (
                 weight[place + 2, :, cols] * grad_f
             ).astype(BF16)
-        products = mm(q[:, cols], scaled[h], TN)
+        products = mm(q_turned[h], scaled[h], NN)
         for place in range(bits):
 
             @pl.when(bit_of(me, place) == 1)
@@ -493,6 +504,31 @@
 
             row_peers(send_row_qg)
             row_qg_in[pl.ds(2 * across, n)] = row_qg[pl.ds(2 * across, n)]
+
+    for h in range(heads):
+        cols = head_cols(h)
+        unit = attn[:, cols].astype(F32) * inv
+        normed[:, cols] = (unit * gain[:, cols]).astype(BF16)
+        gpart[:, cols] = jnp.sum(cot[:, cols].astype(F32) * unit, axis=0, keepdims=True)
+
+    def send_gain(place, peer):
+        send(gpart, gpart_in.at[across], send_sem.at[6], recv_sem.at[6], "seq", peer)
+
+    row_peers(send_gain)
+    gpart_in[across] = gpart[...]
+
+    def send_normed(peer):
+        send(
+            normed.at[pl.ds(pl.multiple_of(peer * piece, piece), piece)],
+            normed_out.at[:, my_cols],
+            send_sem.at[5],
+            recv_sem.at[5],
+            "head",
+            peer,
+        )
+
+    head_peers(send_normed)
+    normed_out[:, my_cols] = normed[pl.ds(pl.multiple_of(mine * piece, piece), piece), :]
 
     lane_ids = lax.broadcasted_iota(jnp.int32, (8, width), 1) // DH
     head_rows = (
@@ -508,38 +544,13 @@
         tpart[l] = result[0:heads, :]
     for l in range(levels):
 
-        @pl.when(me != l)
-        def _():
-            send(tpart.at[l], tpart_in.at[me], send_sem.at[7], recv_sem.at[7], "seq", l)
-
-        @pl.when(me == l)
+        @pl.when(me != owner[l])
+        def _():
+            send(tpart.at[l], tpart_in.at[me], send_sem.at[7], recv_sem.at[7], "seq", owner[l])
+
+        @pl.when(me == owner[l])
         def _():
             tpart_in[me] = tpart[l]
-
-    for h in range(heads):
-        cols = head_cols(h)
-        unit = attn[:, cols].astype(F32) * inv
-        normed[:, cols] = (unit * gain[:, cols]).astype(BF16)
-        gpart[:, cols] = jnp.sum(cot[:, cols].astype(F32) * unit, axis=0, keepdims=True)
-
-    def send_gain(place, peer):
-        send(gpart, gpart_in.at[across], send_sem.at[6], recv_sem.at[6], "seq", peer)
-
-    row_peers(send_gain)
-    gpart_in[across] = gpart[...]
-
-    def send_normed(peer):
-        send(
-            normed.at[pl.ds(pl.multiple_of(peer * piece, piece), piece)],
-            normed_out.at[:, my_cols],
-            send_sem.at[5],
-            recv_sem.at[5],
-            "head",
-            peer,
-        )
-
-    head_peers(send_normed)
-    normed_out[:, my_cols] = normed[pl.ds(pl.multiple_of(mine * piece, piece), piece), :]
 
     for h in range(heads):
         cols = head_cols(h)
@@ -558,23 +569,54 @@
             dq[at] = value.astype(BF16)
             dk[at] = mm(grad_scores, q[at], TN)
             dv[at] = mm(weighted[2 * h + i], grad_h[span_rows(i)], TN)
-
-    drain(gpart_in.at[0 : NX - 1], recv_sem.at[6])
-    both = gpart_in[0]
-    for c in range(1, NX):
-        both = both + gpart_in[c]
-    gline[...] = both
-    gline_in[down] = both
-    for offset in range(1, lines):
-        line = lax.rem(down + offset, jnp.int32(lines))
-        send(
-            gline,
-            gline_in.at[down],
-            send_sem.at[14],
-            recv_sem.at[14],
-            "seq",
-            line * NX + across,
-        )
+        if h == 1:
+            drain(gpart_in.at[0 : NX - 1], recv_sem.at[6])
+            both = gpart_in[0]
+            for c in range(1, NX):
+                both = both + gpart_in[c]
+            gline[...] = both
+            gline_in[down] = both
+            for offset in range(1, lines):
+                line = lax.rem(down + offset, jnp.int32(lines))
+                send(
+                    gline,
+                    gline_in.at[down],
+                    send_sem.at[14],
+                    recv_sem.at[14],
+                    "seq",
+                    line * NX + across,
+                )
+
+
+    for n in (0, 1, 2):
+
+        @pl.when(row_count == n)
+        def _():
+            drain(row_qg_in.at[0 : NX - n], recv_sem.at[13])
+
+    both = row_qg_in[4].astype(F32) + row_qg_in[7].astype(F32)
+    row_ks[0] = (row_qg_in[2].astype(F32) + both).astype(BF16)
+    row_ks[1] = both.astype(BF16)
+    row_ks[2] = row_qg_in[6]
+    row_ks[3] = jnp.zeros((DH, DH), BF16)
+    row_ks_in[across] = row_ks[across]
+    for place in range(NX - 1):
+
+        @pl.when(across != place)
+        def _():
+            send(
+                row_ks.at[place],
+                row_ks_in.at[across],
+                send_sem.at[15],
+                recv_sem.at[15],
+                "seq",
+                down * NX + place,
+            )
+
+    @pl.when(across == NX - 1)
+    def _():
+        for place in range(NX - 1):
+            row_ks_in[place] = jnp.zeros((DH, DH), BF16)
 
     for n in range(0, far_bits + 1):
 
@@ -612,36 +654,6 @@
     seq_peers(send_ks)
     ks_in[me] = ks[me]
 
-    for n in (0, 1, 2):
-
-        @pl.when(row_count == n)
-        def _():
-            drain(row_qg_in.at[0 : NX - n], recv_sem.at[13])
-
-    both = row_qg_in[4].astype(F32) + row_qg_in[7].astype(F32)
-    row_ks[0] = (row_qg_in[2].astype(F32) + both).astype(BF16)
-    row_ks[1] = both.astype(BF16)
-    row_ks[2] = row_qg_in[6]
-    row_ks[3] = jnp.zeros((DH, DH), BF16)
-    row_ks_in[across] = row_ks[across]
-    for place in range(NX - 1):
-
-        @pl.when(across != place)
-        def _():
-            send(
-                row_ks.at[place],
-                row_ks_in.at[across],
-                send_sem.at[15],
-                recv_sem.at[15],
-                "seq",
-                down * NX + place,
-            )
-
-    @pl.when(across == NX - 1)
-    def _():
-        for place in range(NX - 1):
-            row_ks_in[place] = jnp.zeros((DH, DH), BF16)
-
     if lines > 1:
         drain(gline_in.at[0 : lines - 1], recv_sem.at[14])
     both = gline_in[0]
@@ -657,7 +669,7 @@
 
     for l in range(levels):
 
-        @pl.when(me == l)
+        @pl.when(me == owner[l])
         def _():
             drain(tpart_in.at[0 : shards - 1], recv_sem.at[7])
             both = tpart_in[0]
@@ -689,7 +701,7 @@
     drain(gall.at[:, 0 : features - width], recv_sem.at[8])
     for l in range(levels):
 
-        @pl.when(me != l)
+        @pl.when(me != owner[l])
         def _():
             drain(tsum.at[l], tab_sem.at[l])
 
@@ -729,12 +741,14 @@
     drain(gall.at[:, 0 : features - width], send_sem.at[8])
     drain(ks_in.at[0 : shards - 1], send_sem.at[9])
 
-    @pl.when(me < levels)
+    is_owner = functools.reduce(lambda a, b: a | b, [me == owner[l] for l in range(levels)])
+
+    @pl.when(is_owner)
     def _():
         drain(tpart.at[0 : levels - 1], send_sem.at[7])
         drain(tpart_in.at[0 : shards - 1], send_sem.at[10])
 
-    @pl.when(me >= levels)
+    @pl.when(jnp.logical_not(is_owner))
     def _():
         drain(tpart, send_sem.at[7])
 
@@ -818,6 +832,7 @@
             vmem((NX, DH, DH), BF16),
             vmem((1, width), F32),
             vmem((shards // NX, 1, width), F32),
+            vmem((heads, DH, toks), BF16),
             pltpu.SemaphoreType.DMA((7,)),
             pltpu.SemaphoreType.DMA((16,)),
             pltpu.SemaphoreType.DMA((16,)),

time: 57.2 us -> 56.2 us (0.983)
  Pallas kernels: 56.4 us -> 55.2 us
    pallas_call x1, Pallas kernels: 55.4 us -> 54.1 us  [body(): pl.pallas_call(functools.partial(kernel, shards, members), out_shape=(jax...]
where the time goes in v4:
time: 56.2 us; the launch traced here: 55.8 us
  Pallas kernels  55.2 us (98%)
  between operations  0.64 us (1%)
    pallas_call x1, Pallas kernels, body(): pl.pallas_call(functools.partial(kernel, shards, members), out_shape=(jax...  54.1 us

profile of v4, /device:TPU:1, one launch (start us, length us, event | category | flops | bytes accessed | tf_op | source)
XLA Modules:
  0.0 55.8 jit_solution(4320797986847978325)
XLA Ops:
  0.6 54.1 %shard_map.118 = (bf16[16,8192]{1,0:T(8,128)(2,1)S(1)}, bf16[256,512]{1,0:T(8,128)(2,1)S(1)}, bf16[256,512]{1,0:T(8,128)(2,1)S(1)}, bf16[256,512]{1,0:T(8,128)(2...) custom-call(bf16[256,512]{1,0:T(8,128)(2,1)} %q_in.1, bf16[256,512]{1,0:T(8,128)(2,1)} %k_in.1, ...), custom_call_target="tpu_custom_call" | custom-call | tf_op jit(solution)/shard_map/pallas_call | solution.py:776
  54.8 1.0 %shard_map.119 = (bf16[16,8192]{1,0:T(8,128)(2,1)}, bf16[256,512]{1,0:T(8,128)(2,1)}, bf16[256,512]{1,0:T(8,128)(2,1)}, bf16[256,512]{1,0:T(8,128)(2,1)}, f32[7,4,64]{2,1,0:T(4,128)}, /*index=5*/f32[1,8192]{1,0:T(1,128)}) custom-call(bf16[16,8192]{1,0:T(8,128)(2,1)S(1)} %get-tuple-element.18.refs_0_, bf16[256,512]{1,0:T(8,128)(2,1)S(1)} %get-tuple-element.19.refs_1_, ...), custom_call_target="tpu_custom_call" | custom-call | tf_op jit(solution)/shard_map/pallas_call | solution.py:858

commit v5 on v4

--- a/solution.py
+++ b/solution.py
@@ -231,7 +231,10 @@
             peer,
         )
 
-    seq_peers(send_total)
+    @pl.when(down != lines - 1)
+    def _():
+        seq_peers(send_total)
+
 
     def send_row(place, peer):
         send(
@@ -292,7 +295,14 @@
             q[span_rows(1), head_cols(h)], intra[h], NN
         )
 
-    drain(total_in.at[0 : shards - 1], recv_sem.at[0])
+    @pl.when(down != lines - 1)
+    def _():
+        drain(total_in.at[0 : shards - NX - 1], recv_sem.at[0])
+
+    @pl.when(down == lines - 1)
+    def _():
+        drain(total_in.at[0 : shards - NX], recv_sem.at[0])
+
     sums = [
         functools.reduce(
             lambda a, b: a + b,
@@ -649,10 +659,18 @@
             ks[c] = block
 
     def send_ks(peer):
-        send(ks.at[peer], ks_in.at[me], send_sem.at[9], recv_sem.at[9], "seq", peer)
+        @pl.when(lax.div(peer, jnp.int32(NX)) != lines - 1)
+        def _():
+            send(ks.at[peer], ks_in.at[me], send_sem.at[9], recv_sem.at[9], "seq", peer)
 
     seq_peers(send_ks)
-    ks_in[me] = ks[me]
+    @pl.when(down != lines - 1)
+    def _():
+        ks_in[me] = ks[me]
+
+    @pl.when(down == lines - 1)
+    def _():
+        ks_in[...] = jnp.zeros_like(ks_in)
 
     if lines > 1:
         drain(gline_in.at[0 : lines - 1], recv_sem.at[14])
@@ -682,7 +700,9 @@
 
             seq_peers(send_tsum)
 
-    drain(ks_in.at[0 : shards - 1], recv_sem.at[9])
+    @pl.when(down != lines - 1)
+    def _():
+        drain(ks_in.at[0 : shards - 1], recv_sem.at[9])
 
     @pl.when(across != NX - 1)
     def _():
@@ -706,7 +726,10 @@
             drain(tsum.at[l], tab_sem.at[l])
 
     drain(normed_out.at[:, 0 : features - width], recv_sem.at[5])
-    drain(total.at[0 : (shards - 1) * rows], send_sem.at[0])
+    @pl.when(down != lines - 1)
+    def _():
+        drain(total.at[0 : (shards - 1) * rows], send_sem.at[0])
+
     drain(cot.at[0 : toks - piece], send_sem.at[1])
     drain(stat_in.at[0 : members - 1], send_sem.at[3])
     for n in range(0, far_bits + 1):
@@ -739,7 +762,13 @@
     drain(normed.at[0 : toks - piece], send_sem.at[5])
     drain(gpart_in.at[0 : NX - 1], send_sem.at[6])
     drain(gall.at[:, 0 : features - width], send_sem.at[8])
-    drain(ks_in.at[0 : shards - 1], send_sem.at[9])
+    @pl.when(down != lines - 1)
+    def _():
+        drain(ks_in.at[0 : shards - NX - 1], send_sem.at[9])
+
+    @pl.when(down == lines - 1)
+    def _():
+        drain(ks_in.at[0 : shards - NX], send_sem.at[9])
 
     is_owner = functools.reduce(lambda a, b: a | b, [me == owner[l] for l in range(levels)])
 

time: 56.2 us -> 56.3 us (level)
  no operation moved by 1% of the time
where the time goes in v5:
time: 56.3 us; the launch traced here: 55.8 us
  Pallas kernels  55.1 us (98%)
  between operations  0.64 us (1%)
    pallas_call x1, Pallas kernels, body(): pl.pallas_call(functools.partial(kernel, shards, members), out_shape=(jax...  54.1 us

profile of v5, /device:TPU:1, one launch (start us, length us, event | category | flops | bytes accessed | tf_op | source)
XLA Modules:
  0.0 55.8 jit_solution(16138532659519680228)
XLA Ops:
  0.6 54.1 %shard_map.118 = (bf16[16,8192]{1,0:T(8,128)(2,1)S(1)}, bf16[256,512]{1,0:T(8,128)(2,1)S(1)}, bf16[256,512]{1,0:T(8,128)(2,1)S(1)}, bf16[256,512]{1,0:T(8,128)(2...) custom-call(bf16[256,512]{1,0:T(8,128)(2,1)} %q_in.1, bf16[256,512]{1,0:T(8,128)(2,1)} %k_in.1, ...), custom_call_target="tpu_custom_call" | custom-call | tf_op jit(solution)/shard_map/pallas_call | solution.py:805
  54.8 1.0 %shard_map.119 = (bf16[16,8192]{1,0:T(8,128)(2,1)}, bf16[256,512]{1,0:T(8,128)(2,1)}, bf16[256,512]{1,0:T(8,128)(2,1)}, bf16[256,512]{1,0:T(8,128)(2,1)}, f32[7,4,64]{2,1,0:T(4,128)}, /*index=5*/f32[1,8192]{1,0:T(1,128)}) custom-call(bf16[16,8192]{1,0:T(8,128)(2,1)S(1)} %get-tuple-element.18.refs_0_, bf16[256,512]{1,0:T(8,128)(2,1)S(1)} %get-tuple-element.19.refs_1_, ...), custom_call_target="tpu_custom_call" | custom-call | tf_op jit(solution)/shard_map/pallas_call | solution.py:887
